TPU v7x, 128 devices: a whole 4x4x4 slice. The times are simulated.
128 devices in a mesh: dp: 2 (over x_hi), expert: 64 (over z, x_lo, y, core).
Axes of the slice: x: 4 (x_hi: 2, x_lo: 2; x = x_hi * 2 + x_lo), y: 4, z: 4, core: 2. Of those that a mesh axis runs over, the one named last changes fastest.
Arguments:
- tokens: bfloat16 [16384, 2048], P(('dp', 'expert')), may hold values from -6 to 6
- routes: int32 [16384, 4], P(('dp', 'expert')), may hold values from 0 to 63, all different within a row; in each aligned block of 128 rows (0 to 127, 128 to 255, ...) at most 16 rows name the same one
- route_gates: bfloat16 [16384, 4], P(('dp', 'expert')), may hold values from 0.049804688 to 1
- cotangent: bfloat16 [16384, 2048], P(('dp', 'expert')), may hold values from -3 to 3
- swap_pairs: int32 [32, 2], replicated, may hold values from 0 to 63, as said below
- w_gate: bfloat16 [64, 2048, 768], P('expert'), may hold values from -0.125 to 0.125
- w_up: bfloat16 [64, 2048, 768], P('expert'), may hold values from -0.125 to 0.125
- w_down: bfloat16 [64, 768, 2048], P('expert'), may hold values from -0.21875 to 0.21875
- moment_first: bfloat16 [64, 768, 2048], P('expert', 'dp'), may hold values from -6 to 6
- moment_second: bfloat16 [64, 768, 2048], P('expert', 'dp'), may hold values from 0.099609375 to 4
Outputs:
- combined: bfloat16 [16384, 2048], P(('dp', 'expert'))
- new_gate: bfloat16 [64, 2048, 768], P('expert', None, 'dp')
- new_up: bfloat16 [64, 2048, 768], P('expert', None, 'dp')
- new_down: bfloat16 [64, 768, 2048], P('expert', 'dp')
- new_first: bfloat16 [64, 768, 2048], P('expert', 'dp')
- new_second: bfloat16 [64, 768, 2048], P('expert', 'dp')
- adam_step: bfloat16 [64, 768, 2048], P('expert', 'dp')
Inputs may be any that keep to these rules, and one draw needn't show every extreme that they name: `routes`: each aligned block of 128 tokens (the tokens of one device) names no expert more than 16 times, and some block names some expert exactly 16 times; each token names 4 different experts. `swap_pairs`: every device index of the expert axis appears exactly once, so every device trades its expert with one other.
All inputs are finite; a program needn't handle non-finite values.
Results may differ from a plain program's by a relative error of at most 0.014.
Values may be sent and summed in bfloat16 or wider, within the bound.
No kernel may reach another device: no remote copies, remote signals or barrier semaphores. Data moves between devices by JAX's collectives and lax.ppermute only.
A program may use at most 192 MiB of HBM per device.

v0:
```python
import jax
import jax.numpy as jnp
from jax import lax
from jax.sharding import PartitionSpec as P

beta_first = 0.9
beta_second = 0.95
adam_eps = 1e-08


def partners(swap_pairs, count):
    slot_ids = jnp.arange(count, dtype=jnp.int32)
    pair_left = swap_pairs[:, 0:1]
    pair_right = swap_pairs[:, 1:2]
    offsets = jnp.where(pair_left == slot_ids[None, :], pair_right - slot_ids[None, :], 0)
    offsets = offsets + jnp.where(pair_right == slot_ids[None, :], pair_left - slot_ids[None, :], 0)
    return slot_ids + jnp.sum(offsets, axis=0)


def adam_update(first_in, second_in, grad_half):
    first_moment = beta_first * first_in.astype(jnp.float32) + (1.0 - beta_first) * grad_half
    second_moment = (
        beta_second * second_in.astype(jnp.float32) + (1.0 - beta_second) * grad_half * grad_half
    )
    direction = first_moment / (jnp.sqrt(second_moment) + adam_eps)
    return (
        first_moment.astype(jnp.bfloat16),
        second_moment.astype(jnp.bfloat16),
        direction.astype(jnp.bfloat16),
    )


def flat_rows(members, owners_count):
    return [member.reshape(owners_count, -1) for member in members]


def relocate_state(gate_part, up_part, down_part, first_part, second_part, partner):
    owners_count = lax.axis_size("expert")
    members = (gate_part, up_part, down_part, first_part, second_part)
    rows = flat_rows(members, owners_count)
    spread = (
        lax.all_to_all(rows[0], "expert", split_axis=0, concat_axis=0, tiled=True),
        lax.all_to_all(rows[1], "expert", split_axis=0, concat_axis=0, tiled=True),
        lax.all_to_all(rows[2], "expert", split_axis=0, concat_axis=0, tiled=True),
        lax.all_to_all(rows[3], "expert", split_axis=0, concat_axis=0, tiled=True),
        lax.all_to_all(rows[4], "expert", split_axis=0, concat_axis=0, tiled=True),
    )
    ordered = [jnp.take(member, partner, axis=0) for member in spread]
    landed = (
        lax.all_to_all(ordered[0], "expert", split_axis=0, concat_axis=0, tiled=True),
        lax.all_to_all(ordered[1], "expert", split_axis=0, concat_axis=0, tiled=True),
        lax.all_to_all(ordered[2], "expert", split_axis=0, concat_axis=0, tiled=True),
        lax.all_to_all(ordered[3], "expert", split_axis=0, concat_axis=0, tiled=True),
        lax.all_to_all(ordered[4], "expert", split_axis=0, concat_axis=0, tiled=True),
    )
    return [piece.reshape(member.shape) for piece, member in zip(landed, members)]


def run_layer(tokens, routes, route_gates, cotangent, owner, gate_w, up_w, down_w):
    owners_count = lax.axis_size("expert")
    tok_dev, fanout = routes.shape
    width = tokens.shape[1]
    capacity = 2 * tok_dev * fanout // owners_count
    flat_ids = routes.reshape(-1)
    rows_count = flat_ids.shape[0]
    onehot = (flat_ids[:, None] == jnp.arange(owners_count, dtype=jnp.int32)[None, :]).astype(
        jnp.int32
    )
    slot_rank = jnp.sum((jnp.cumsum(onehot, axis=0) - onehot) * onehot, axis=1)
    target = jnp.sum(onehot * owner[None, :], axis=1)
    position = target * capacity + slot_rank
    source = (
        jnp.full((owners_count * capacity,), -1, jnp.int32)
        .at[position]
        .set(jnp.arange(rows_count, dtype=jnp.int32))
    )
    filled = source >= 0
    source_row = jnp.where(filled, source, 0)
    token_of = source_row // fanout
    zero_rows = jnp.zeros((), jnp.bfloat16)
    send_x = jnp.where(filled[:, None], tokens[token_of], zero_rows).reshape(
        owners_count, capacity, width
    )
    send_dy = jnp.where(filled[:, None], cotangent[token_of], zero_rows).reshape(
        owners_count, capacity, width
    )
    send_gate = jnp.where(filled, route_gates.reshape(-1)[source_row], zero_rows).reshape(
        owners_count, capacity
    )
    rows_x = lax.all_to_all(send_x, "expert", split_axis=0, concat_axis=0, tiled=True)
    rows_dy = lax.all_to_all(send_dy, "expert", split_axis=0, concat_axis=0, tiled=True)
    rows_gate = lax.all_to_all(send_gate, "expert", split_axis=0, concat_axis=0, tiled=True)
    senders, items = rows_gate.shape
    flat_x = rows_x.reshape(senders * items, width)
    gate_pre = jnp.dot(flat_x, gate_w, preferred_element_type=jnp.float32)
    up_pre = jnp.dot(flat_x, up_w, preferred_element_type=jnp.float32)
    hidden = (jax.nn.silu(gate_pre) * up_pre).astype(jnp.bfloat16)
    outputs = jnp.dot(hidden, down_w, preferred_element_type=jnp.float32).astype(jnp.bfloat16)
    scaled = (
        rows_gate.reshape(-1, 1).astype(jnp.float32)
        * rows_dy.reshape(-1, width).astype(jnp.float32)
    ).astype(jnp.bfloat16)
    returned = lax.all_to_all(
        outputs.reshape(senders, items, width), "expert", split_axis=0, concat_axis=0, tiled=True
    )
    returned, hidden, scaled = (
        returned,
        hidden.reshape(senders, items, -1),
        scaled.reshape(senders, items, width),
    )
    picked = returned.reshape(-1, width)[position].reshape(tok_dev, fanout, width)
    combined = jnp.sum(
        picked.astype(jnp.float32) * route_gates.astype(jnp.float32)[:, :, None], axis=1
    ).astype(jnp.bfloat16)
    hidden_flat = hidden.reshape(owners_count * capacity, -1)
    scaled_flat = scaled.reshape(owners_count * capacity, width)
    grad_half = lax.psum_scatter(
        lax.dot_general(
            hidden_flat, scaled_flat, (((0,), (0,)), ((), ())), preferred_element_type=jnp.float32
        ).astype(jnp.bfloat16),
        "dp",
        scatter_dimension=0,
        tiled=True,
    ).astype(jnp.float32)
    return (combined, grad_half)


def local(
    tokens,
    routes,
    route_gates,
    cotangent,
    swap_pairs,
    w_gate,
    w_up,
    w_down,
    moment_first,
    moment_second,
):
    owners_count = lax.axis_size("expert")
    replica = lax.axis_index("dp")
    partner = partners(swap_pairs, owners_count)
    half_rows = w_gate.shape[2] // lax.axis_size("dp")
    relocated = relocate_state(w_gate, w_up, w_down, moment_first, moment_second, partner)
    combined, grad_half = run_layer(
        tokens,
        routes,
        route_gates,
        cotangent,
        partner,
        relocated[0][0],
        relocated[1][0],
        relocated[2][0],
    )
    first_out, second_out, step_out = adam_update(relocated[3][0], relocated[4][0], grad_half)
    new_gate = lax.dynamic_slice_in_dim(relocated[0], replica * half_rows, half_rows, 2)
    new_up = lax.dynamic_slice_in_dim(relocated[1], replica * half_rows, half_rows, 2)
    new_down = lax.dynamic_slice_in_dim(relocated[2], replica * half_rows, half_rows, 1)
    new_first = first_out[None]
    new_second = second_out[None]
    adam_step = step_out[None]
    return (combined, new_gate, new_up, new_down, new_first, new_second, adam_step)


def solution(mesh):
    placed = (
        P(("dp", "expert"), None),
        P(("dp", "expert"), None),
        P(("dp", "expert"), None),
        P(("dp", "expert"), None),
        P(),
        P("expert", None, None),
        P("expert", None, None),
        P("expert", None, None),
        P("expert", "dp", None),
        P("expert", "dp", None),
    )
    return jax.shard_map(
        local,
        mesh=mesh,
        in_specs=placed,
        out_specs=(
            P(("dp", "expert"), None),
            P("expert", None, "dp"),
            P("expert", None, "dp"),
            P("expert", "dp", None),
            P("expert", "dp", None),
            P("expert", "dp", None),
            P("expert", "dp", None),
        ),
        check_vma=False,
    )
```

profile of v0, /device:TPU:1, one launch (start us, length us, event | category | flops | bytes accessed | tf_op | source)
XLA Modules:
  0.0 860.3 jit_solution(7380569915248814662)
XLA Ops:
  21.8 11.2 %all-to-all-start.10 = ((bf16[64,1,16]{2,1,0:T(2,128)(2,1)}), bf16[64,1,16]{2,1,0:T(2,128)(2,1)S(1)}, u32[]{:S(2)}, u32[]{:S(2)}) async-start(bf16[64,1,16]{2,1,0:T(2,128)(2,1)} %all_to_all.119), calls=%async_computation.10 | async-start | bytes 65536 | tf_op jit(solution)/shard_map/all_to_all | solution.py:92
  38.1 11.8 %reduce.23 = bf16[64,12288]{1,0:T(8,128)(2,1)S(1)} reduce(bf16[64,1,12288]{2,1,0:T(2,128)(2,1)} %all_to_all.118, bf16[]{:T(256)} %broadcast.129), dimensions={1}, to_apply=%all_to_all.118.reduce_sub_computation | reduce | bytes 3145730 | tf_op jit(solution)/shard_map/all_to_all | solution.py:45
  66.1 11.8 %reduce.22 = bf16[64,12288]{1,0:T(8,128)(2,1)S(1)} reduce(bf16[64,1,12288]{2,1,0:T(2,128)(2,1)} %all_to_all.120, bf16[]{:T(256)} %broadcast.129), dimensions={1}, to_apply=%all_to_all.120.reduce_sub_computation | reduce | bytes 3145730 | tf_op jit(solution)/shard_map/all_to_all | solution.py:46
  90.0 16.0 %all_to_all.116 = bf16[64,1,24576]{2,1,0:T(2,128)(2,1)} reshape(bf16[1,2048,768]{2,1,0:T(8,128)(2,1)} %param.20) | data formatting | bytes 6291456 | tf_op jit(solution)/shard_map/all_to_all | solution.py:43
  105.9 20.6 %reduce.17 = bf16[64,24576]{1,0:T(8,128)(2,1)} reduce(bf16[64,1,24576]{2,1,0:T(2,128)(2,1)} %all_to_all.116, bf16[]{:T(256)} %broadcast.129), dimensions={1}, to_apply=%all_to_all.116.reduce_sub_computation | reduce | bytes 6291458 | tf_op jit(solution)/shard_map/all_to_all | solution.py:43
  141.9 12.4 %all_to_all.117 = bf16[64,1,24576]{2,1,0:T(2,128)(2,1)} reshape(bf16[1,768,2048]{2,1,0:T(8,128)(2,1)} %param.21) | data formatting | bytes 6291456 | tf_op jit(solution)/shard_map/all_to_all | solution.py:44
  154.3 20.6 %reduce.16 = bf16[64,24576]{1,0:T(8,128)(2,1)} reduce(bf16[64,1,24576]{2,1,0:T(2,128)(2,1)} %all_to_all.117, bf16[]{:T(256)} %broadcast.129), dimensions={1}, to_apply=%all_to_all.117.reduce_sub_computation | reduce | bytes 6291458 | tf_op jit(solution)/shard_map/all_to_all | solution.py:44
  189.3 16.0 %all_to_all.115 = bf16[64,1,24576]{2,1,0:T(2,128)(2,1)} reshape(bf16[1,2048,768]{2,1,0:T(8,128)(2,1)} %param.19) | data formatting | bytes 6291456 | tf_op jit(solution)/shard_map/all_to_all | solution.py:42
  205.2 20.6 %reduce.18 = bf16[64,24576]{1,0:T(8,128)(2,1)} reduce(bf16[64,1,24576]{2,1,0:T(2,128)(2,1)} %all_to_all.115, bf16[]{:T(256)} %broadcast.129), dimensions={1}, to_apply=%all_to_all.115.reduce_sub_computation | reduce | bytes 6291458 | tf_op jit(solution)/shard_map/all_to_all | solution.py:42
  325.6 17.4 %reshape.306 = bf16[64,1,24576]{2,1,0:T(2,128)(2,1)} reshape(bf16[64,2,12288]{2,1,0:T(2,128)(2,1)} %all-to-all-done.3) | data formatting | bytes 6291456
  353.5 17.4 %reshape.310 = bf16[64,1,24576]{2,1,0:T(2,128)(2,1)} reshape(bf16[64,2,12288]{2,1,0:T(2,128)(2,1)} %all-to-all-done.5) | data formatting | bytes 6291456
  381.3 17.6 %reshape.302 = bf16[64,1,24576]{2,1,0:T(2,128)(2,1)} reshape(bf16[64,2,12288]{2,1,0:T(2,128)(2,1)} %all-to-all-done.1) | data formatting | bytes 6291456
  433.0 40.7 %all-to-all-done.11 = bf16[64,16,2048]{2,1,0:T(8,128)(2,1)} async-done(((bf16[64,16,2048]{2,1,0:T(8,128)(2,1)}), bf16[64,16,2048]{2,1,0:T(8,128)(2,1)}, u32[]{:S(2)}, u32[]{:S(2)}) %all-to-all-start.11) | async-done | bytes 4194336 | tf_op jit(solution)/shard_map/all_to_all | solution.py:91
  487.6 32.1 %all-to-all-done.2 = bf16[64,2,12288]{2,1,0:T(2,128)(2,1)} async-done(((bf16[64,2,12288]{2,1,0:T(2,128)(2,1)}), bf16[64,2,12288]{2,1,0:T(2,128)(2,1)}, u32[]{:S(2)}, u32[]{:S(2)}) %all-to-all-start.2) | async-done | bytes 3145760 | tf_op jit(solution)/shard_map/all_to_all | solution.py:50
  533.5 32.9 %all-to-all-done.4 = bf16[64,2,12288]{2,1,0:T(2,128)(2,1)} async-done(((bf16[64,2,12288]{2,1,0:T(2,128)(2,1)}), bf16[64,2,12288]{2,1,0:T(2,128)(2,1)}, u32[]{:S(2)}, u32[]{:S(2)}) %all-to-all-start.4) | async-done | bytes 3145760 | tf_op jit(solution)/shard_map/all_to_all | solution.py:51
  571.8 17.8 %reshape.304 = bf16[64,1,24576]{2,1,0:T(2,128)(2,1)} reshape(bf16[64,2,12288]{2,1,0:T(2,128)(2,1)} %all-to-all-done.2) | data formatting | bytes 6291456
  589.6 18.3 %reduce.1 = bf16[64,24576]{1,0:T(8,128)(2,1)S(1)} reduce(bf16[64,1,24576]{2,1,0:T(2,128)(2,1)} %reshape.304, bf16[]{:T(256)} %constant.86), dimensions={1}, to_apply=%all_to_all.90.reduce_sub_computation | reduce | bytes 6291458 | tf_op jit(solution)/shard_map/all_to_all | solution.py:50
  610.8 17.4 %reshape.308 = bf16[64,1,24576]{2,1,0:T(2,128)(2,1)} reshape(bf16[64,2,12288]{2,1,0:T(2,128)(2,1)} %all-to-all-done.4) | data formatting | bytes 6291456
  628.2 19.9 %reduce.2 = bf16[64,24576]{1,0:T(8,128)(2,1)} reduce(bf16[64,1,24576]{2,1,0:T(2,128)(2,1)} %reshape.308, bf16[]{:T(256)} %constant.86), dimensions={1}, to_apply=%all_to_all.95.reduce_sub_computation | reduce | bytes 6291458 | tf_op jit(solution)/shard_map/all_to_all | solution.py:51
  691.6 17.4 %reshape.312 = bf16[64,1,24576]{2,1,0:T(2,128)(2,1)} reshape(bf16[64,2,12288]{2,1,0:T(2,128)(2,1)} %all-to-all-done.6) | data formatting | bytes 6291456
  709.0 20.0 %reduce.3 = bf16[64,24576]{1,0:T(8,128)(2,1)} reduce(bf16[64,1,24576]{2,1,0:T(2,128)(2,1)} %reshape.312, bf16[]{:T(256)} %constant.86), dimensions={1}, to_apply=%all_to_all.100.reduce_sub_computation | reduce | bytes 6291458 | tf_op jit(solution)/shard_map/all_to_all | solution.py:52
  764.1 13.2 %multiply_reduce_fusion.1 = f32[64,12288]{1,0:T(8,128)} fusion(bf16[64,1,12288]{2,1,0:T(2,128)(2,1)} %reshape.320), kind=kLoop, calls=%fused_computation.30 | loop fusion | flops 1572864 | bytes 4718592 | tf_op jit(solution)/shard_map/mul | solution.py:23
  781.6 10.5 %reshape.316 = bf16[64,1,12288]{2,1,0:T(2,128)(2,1)} reshape(bf16[64,2,6144]{2,1,0:T(2,128)(2,1)} %all-to-all-done.9) | data formatting | bytes 3145728
  792.1 13.2 %multiply_reduce_fusion.2 = f32[64,12288]{1,0:T(8,128)} fusion(bf16[64,1,12288]{2,1,0:T(2,128)(2,1)} %reshape.316), kind=kLoop, calls=%fused_computation.31 | loop fusion | flops 1572864 | bytes 4718592 | tf_op jit(solution)/shard_map/mul | solution.py:21
  (143 shorter events, 399.1 us)
Async XLA Ops:
  7.2 288.2 %copy-start = (bf16[128,2048]{1,0:T(8,128)(2,1)S(1)}, bf16[128,2048]{1,0:T(8,128)(2,1)}, u32[]{:S(2)}) copy-start(bf16[128,2048]{1,0:T(8,128)(2,1)} %param.17) | copy-start | bytes 1572868
  7.2 25.9 %copy-start.10 = (bf16[1,384,2048]{2,1,0:T(8,128)(2,1)S(1)}, bf16[1,384,2048]{2,1,0:T(8,128)(2,1)}, u32[]{:S(2)}) copy-start(bf16[1,384,2048]{2,1,0:T(8,128)(2,1)} %param.22) | copy-start | bytes 4718596
  21.8 30.1 %all-to-all-start.10 = ((bf16[64,1,16]{2,1,0:T(2,128)(2,1)}), bf16[64,1,16]{2,1,0:T(2,128)(2,1)S(1)}, u32[]{:S(2)}, u32[]{:S(2)}) async-start(bf16[64,1,16]{2,1,0:T(2,128)(2,1)} %all_to_all.119), calls=%async_computation.10 | async-start | bytes 65536 | tf_op jit(solution)/shard_map/all_to_all | solution.py:92
  52.0 9.6 %copy-start.11 = (bf16[1,384,2048]{2,1,0:T(8,128)(2,1)S(1)}, bf16[1,384,2048]{2,1,0:T(8,128)(2,1)}, u32[]{:S(2)}) copy-start(bf16[1,384,2048]{2,1,0:T(8,128)(2,1)} %param.23) | copy-start | bytes 4718596
  52.0 32.7 %all-to-all-start.8 = ((bf16[64,2,6144]{2,1,0:T(2,128)(2,1)}), bf16[64,2,6144]{2,1,0:T(2,128)(2,1)}, u32[]{:S(2)}, u32[]{:S(2)}) async-start(bf16[64,2,6144]{2,1,0:T(2,128)(2,1)} %reshape.313), calls=%async_computation.8 | async-start | bytes 3145728 | tf_op jit(solution)/shard_map/all_to_all | solution.py:45
  84.7 47.1 %all-to-all-start.12 = ((bf16[64,2,6144]{2,1,0:T(2,128)(2,1)}), bf16[64,2,6144]{2,1,0:T(2,128)(2,1)S(1)}, u32[]{:S(2)}, u32[]{:S(2)}) async-start(bf16[64,2,6144]{2,1,0:T(2,128)(2,1)} %reshape.317), calls=%async_computation.13 | async-start | bytes 3145728 | tf_op jit(solution)/shard_map/all_to_all | solution.py:46
  132.9 50.8 %all-to-all-start.3 = ((bf16[64,2,12288]{2,1,0:T(2,128)(2,1)}), bf16[64,2,12288]{2,1,0:T(2,128)(2,1)}, u32[]{:S(2)}, u32[]{:S(2)}) async-start(bf16[64,2,12288]{2,1,0:T(2,128)(2,1)} %reshape.305), calls=%async_computation.3 | async-start | bytes 6291456 | tf_op jit(solution)/shard_map/all_to_all | solution.py:43
  183.7 47.3 %all-to-all-start.5 = ((bf16[64,2,12288]{2,1,0:T(2,128)(2,1)}), bf16[64,2,12288]{2,1,0:T(2,128)(2,1)}, u32[]{:S(2)}, u32[]{:S(2)}) async-start(bf16[64,2,12288]{2,1,0:T(2,128)(2,1)} %reshape.309), calls=%async_computation.5 | async-start | bytes 6291456 | tf_op jit(solution)/shard_map/all_to_all | solution.py:44
  231.0 55.4 %all-to-all-start.1 = ((bf16[64,2,12288]{2,1,0:T(2,128)(2,1)}), bf16[64,2,12288]{2,1,0:T(2,128)(2,1)}, u32[]{:S(2)}, u32[]{:S(2)}) async-start(bf16[64,2,12288]{2,1,0:T(2,128)(2,1)} %reshape.301), calls=%async_computation.1 | async-start | bytes 6291456 | tf_op jit(solution)/shard_map/all_to_all | solution.py:42
  286.4 32.3 %all-to-all-start.13 = ((bf16[64,2,6144]{2,1,0:T(2,128)(2,1)}), bf16[64,2,6144]{2,1,0:T(2,128)(2,1)S(1)}, u32[]{:S(2)}, u32[]{:S(2)}) async-start(bf16[64,2,6144]{2,1,0:T(2,128)(2,1)} %reshape.319), calls=%async_computation.14 | async-start | bytes 3145728 | tf_op jit(solution)/shard_map/all_to_all | solution.py:54
  295.4 6.0 copy-start.2
  319.9 89.4 %all-to-all-start = ((bf16[64,16,2048]{2,1,0:T(8,128)(2,1)}), bf16[64,16,2048]{2,1,0:T(8,128)(2,1)}, u32[]{:S(2)}, u32[]{:S(2)}) async-start(bf16[64,16,2048]{2,1,0:T(8,128)(2,1)} %get-tuple-element.19), calls=%async_computation | async-start | bytes 8388608 | tf_op jit(solution)/shard_map/all_to_all | solution.py:90
  409.3 9.4 %copy-start.4 = (bf16[64,24576]{1,0:T(8,128)(2,1)S(1)}, bf16[64,24576]{1,0:T(8,128)(2,1)}, u32[]{:S(2)}) copy-start(bf16[64,24576]{1,0:T(8,128)(2,1)} %gather_fusion.5) | copy-start | bytes 9437188
  409.3 64.4 %all-to-all-start.11 = ((bf16[64,16,2048]{2,1,0:T(8,128)(2,1)}), bf16[64,16,2048]{2,1,0:T(8,128)(2,1)}, u32[]{:S(2)}, u32[]{:S(2)}) async-start(bf16[64,16,2048]{2,1,0:T(8,128)(2,1)} %get-tuple-element.18), calls=%async_computation.11 | async-start | bytes 8388608 | tf_op jit(solution)/shard_map/all_to_all | solution.py:91
  473.7 46.0 %all-to-all-start.2 = ((bf16[64,2,12288]{2,1,0:T(2,128)(2,1)}), bf16[64,2,12288]{2,1,0:T(2,128)(2,1)}, u32[]{:S(2)}, u32[]{:S(2)}) async-start(bf16[64,2,12288]{2,1,0:T(2,128)(2,1)} %reshape.303), calls=%async_computation.2 | async-start | bytes 6291456 | tf_op jit(solution)/shard_map/all_to_all | solution.py:50
  519.7 46.7 %all-to-all-start.4 = ((bf16[64,2,12288]{2,1,0:T(2,128)(2,1)}), bf16[64,2,12288]{2,1,0:T(2,128)(2,1)}, u32[]{:S(2)}, u32[]{:S(2)}) async-start(bf16[64,2,12288]{2,1,0:T(2,128)(2,1)} %reshape.307), calls=%async_computation.4 | async-start | bytes 6291456 | tf_op jit(solution)/shard_map/all_to_all | solution.py:51
  566.4 116.2 %all-to-all-start.6 = ((bf16[64,2,12288]{2,1,0:T(2,128)(2,1)}), bf16[64,2,12288]{2,1,0:T(2,128)(2,1)}, u32[]{:S(2)}, u32[]{:S(2)}) async-start(bf16[64,2,12288]{2,1,0:T(2,128)(2,1)} %reshape.311), calls=%async_computation.6 | async-start | bytes 6291456 | tf_op jit(solution)/shard_map/all_to_all | solution.py:52
  571.6 274.6 %reduce-scatter.2.cloned.1.call-start = ((), (), s32[]{:S(2)}) async-start(), calls=%async_computation.15 | async-start | bytes 4718592 | tf_op jit(solution)/shard_map/reduce_scatter | solution.py:117
  652.9 6.3 copy-start.9
  682.6 61.3 %all-to-all-start.9 = ((bf16[64,2,6144]{2,1,0:T(2,128)(2,1)}), bf16[64,2,6144]{2,1,0:T(2,128)(2,1)}, u32[]{:S(2)}, u32[]{:S(2)}) async-start(bf16[64,2,6144]{2,1,0:T(2,128)(2,1)} %reshape.315), calls=%async_computation.9 | async-start | bytes 3145728 | tf_op jit(solution)/shard_map/all_to_all | solution.py:53
  743.9 9.7 %copy-start.14 = (bf16[128,4]{0,1:T(4,128)(2,1)S(1)}, bf16[128,4]{0,1:T(4,128)(2,1)}, u32[]{:S(2)}) copy-start(bf16[128,4]{0,1:T(4,128)(2,1)} %param.16) | copy-start | bytes 3076
  743.9 9.8 %copy-start.13 = (s32[512,1]{0,1:T(1,128)S(1)}, s32[512,1]{0,1:T(1,128)}, u32[]{:S(2)}) copy-start(s32[512,1]{0,1:T(1,128)} %copy-done.12) | copy-start | bytes 6148
  743.9 86.0 %all-to-all-start.7 = ((bf16[64,16,2048]{2,1,0:T(8,128)(2,1)}), bf16[64,16,2048]{2,1,0:T(8,128)(2,1)}, u32[]{:S(2)}, u32[]{:S(2)}) async-start(bf16[64,16,2048]{2,1,0:T(8,128)(2,1)} %bitcast.77), calls=%async_computation.7 | async-start | bytes 8388608 | tf_op jit(solution)/shard_map/all_to_all | solution.py:103
  846.2 7.0 copy-start.1
  (7 other events, 19.8 us)
Sparse Core Ops, SparseCore 0:
  673.9 64.9 reduce-scatter.1
where the time goes:
time: 871 us; the launch traced here: 860 us
  local copies, waits for them, and re-layouts  369 us (42%)
  other arithmetic  222 us (25%)
  waiting for transfers between devices  119 us (14%)
  starting transfers between devices  108 us (12%)
  matrix products  27.4 us (3%)
  between operations  14.7 us (2%)
    unnamed x59, local copies, waits for them, and re-layouts  216 us
    all_to_all x1, waiting for transfers between devices, run_layer(): lax.all_to_all(send_dy, 'expert', split_axis=0, concat_axis=0, tiled=True)  40.7 us
    all_to_all x1, waiting for transfers between devices, relocate_state(): lax.all_to_all(ordered[1], 'expert', split_axis=0, concat_axis=0, tiled=T...  32.9 us
    all_to_all x1, waiting for transfers between devices, relocate_state(): lax.all_to_all(ordered[0], 'expert', split_axis=0, concat_axis=0, tiled=T...  32.1 us
    all_to_all x3, other arithmetic, relocate_state(): lax.all_to_all(ordered[2], 'expert', split_axis=0, concat_axis=0, tiled=T...  30.7 us
    all_to_all x2, other arithmetic, relocate_state(): lax.all_to_all(ordered[1], 'expert', split_axis=0, concat_axis=0, tiled=T...  24.9 us
    all_to_all x2, other arithmetic, relocate_state(): lax.all_to_all(ordered[0], 'expert', split_axis=0, concat_axis=0, tiled=T...  23.3 us
    gather x5, local copies, waits for them, and re-layouts, relocate_state(): ordered = [jnp.take(member, partner, axis=0) for member in spread]  21.2 us
  transfers between devices with their start and end apart: 15, of which 6 were waited for; matrix products, arithmetic and copies ran while one was open for 63% of the time, Pallas kernels for 0%

commit v1 on v0

v1 whole, which is shorter than its diff:
```python
import jax
import jax.numpy as jnp
from jax import lax
from jax.sharding import PartitionSpec as P

beta_first = 0.9
beta_second = 0.95
adam_eps = 1e-08
capacity = 16


def partners(swap_pairs, count):
    slot_ids = jnp.arange(count, dtype=jnp.int32)
    pair_left = swap_pairs[:, 0:1]
    pair_right = swap_pairs[:, 1:2]
    offsets = jnp.where(pair_left == slot_ids[None, :], pair_right - slot_ids[None, :], 0)
    offsets = offsets + jnp.where(pair_right == slot_ids[None, :], pair_left - slot_ids[None, :], 0)
    return slot_ids + jnp.sum(offsets, axis=0)


def to_tiles(array, pieces):
    rows, columns = array.shape
    tiles = array.reshape(rows // 8, 8, columns // 128, 128).transpose(0, 2, 1, 3)
    return tiles.reshape(pieces, -1, 8, 128)


def from_tiles(tiles, rows, columns):
    split = tiles.reshape(rows // 8, columns // 128, 8, 128).transpose(0, 2, 1, 3)
    return split.reshape(rows, columns)


def exchange(array):
    return lax.all_to_all(array, "expert", split_axis=0, concat_axis=0, tiled=True)


def adam_update(first_in, second_in, grad):
    first_moment = beta_first * first_in.astype(jnp.float32) + (1.0 - beta_first) * grad
    second_moment = beta_second * second_in.astype(jnp.float32) + (1.0 - beta_second) * grad * grad
    direction = first_moment / (jnp.sqrt(second_moment) + adam_eps)
    return (
        first_moment.astype(jnp.bfloat16),
        second_moment.astype(jnp.bfloat16),
        direction.astype(jnp.bfloat16),
    )


def slots(routes, route_gates, count):
    tok = routes.shape[0]
    expert_ids = jnp.arange(count, dtype=jnp.int32)
    hits = routes.T[:, None, :] == expert_ids[None, :, None]
    named = jnp.any(hits, axis=0)
    weight = jnp.sum(
        jnp.where(hits, route_gates.T.astype(jnp.float32)[:, None, :], 0.0), axis=0
    )
    earlier = (
        jnp.arange(tok, dtype=jnp.int32)[:, None] < jnp.arange(tok, dtype=jnp.int32)[None, :]
    ).astype(jnp.bfloat16)
    rank = jnp.dot(
        named.astype(jnp.bfloat16), earlier, preferred_element_type=jnp.float32
    ).astype(jnp.int32)
    slot_ids = jnp.arange(capacity, dtype=jnp.int32)
    chosen = named[:, None, :] & (rank[:, None, :] == slot_ids[None, :, None])
    pick = chosen.astype(jnp.bfloat16)
    weigh = jnp.where(chosen, weight[:, None, :], 0.0).astype(jnp.bfloat16)
    return pick, weigh


def local(
    tokens,
    routes,
    route_gates,
    cotangent,
    swap_pairs,
    w_gate,
    w_up,
    w_down,
    moment_first,
    moment_second,
):
    count = lax.axis_size("expert")
    replica = lax.axis_index("dp")
    tok, width = tokens.shape
    partner = partners(swap_pairs, count)
    gate_w, up_w, down_w = w_gate[0], w_up[0], w_down[0]
    ff = gate_w.shape[1]
    half = ff // lax.axis_size("dp")

    pick, weigh = slots(routes, route_gates, count)
    blank = jnp.zeros_like(pick)
    both = jnp.concatenate(
        [jnp.concatenate([pick, blank], axis=2), jnp.concatenate([blank, weigh], axis=2)], axis=1
    )
    rows_out = jnp.dot(
        both.reshape(count * 2 * capacity, 2 * tok),
        jnp.concatenate([tokens, cotangent], axis=0),
        preferred_element_type=jnp.float32,
    ).astype(jnp.bfloat16)
    rows_in = exchange(rows_out.reshape(count, 2 * capacity, width))

    gate_half = lax.dynamic_slice_in_dim(gate_w, replica * half, half, 1)
    up_half = lax.dynamic_slice_in_dim(up_w, replica * half, half, 1)
    down_half = lax.dynamic_slice_in_dim(down_w, replica * half, half, 0)
    state = jnp.concatenate(
        [
            to_tiles(member, count)
            for member in (gate_half, up_half, down_half, moment_first[0], moment_second[0])
        ],
        axis=1,
    )
    state, rows_in = lax.optimization_barrier((state, rows_in))
    spread = exchange(state)

    x_rows = rows_in[:, :capacity].reshape(count * capacity, width)
    scaled = rows_in[:, capacity:].reshape(count * capacity, width)
    gate_pre = jnp.dot(x_rows, gate_w, preferred_element_type=jnp.float32)
    up_pre = jnp.dot(x_rows, up_w, preferred_element_type=jnp.float32)
    hidden = (jax.nn.silu(gate_pre) * up_pre).astype(jnp.bfloat16)
    partial = lax.dot_general(
        hidden, scaled, (((0,), (0,)), ((), ())), preferred_element_type=jnp.float32
    ).astype(jnp.bfloat16)
    kept = lax.dynamic_slice_in_dim(partial, replica * half, half, 0)
    given = lax.dynamic_slice_in_dim(partial, (1 - replica) * half, half, 0)
    taken = lax.ppermute(given, "dp", [(0, 1), (1, 0)])
    outputs = jnp.dot(hidden, down_w, preferred_element_type=jnp.float32).astype(jnp.bfloat16)
    grad = (kept.astype(jnp.float32) + taken.astype(jnp.float32)).astype(jnp.bfloat16)
    answer = jnp.concatenate([to_tiles(outputs, count), to_tiles(grad, count)], axis=1)
    answer, spread = lax.optimization_barrier((answer, spread))
    answered = exchange(answer)

    out_tiles = 2 * (width // 128)
    returned = from_tiles(answered[:, :out_tiles], count * capacity, width)
    combined = lax.dot_general(
        weigh.reshape(count * capacity, tok),
        returned,
        (((0,), (0,)), ((), ())),
        preferred_element_type=jnp.float32,
    ).astype(jnp.bfloat16)

    onward = jnp.concatenate([spread, answered[:, out_tiles:]], axis=1)[partner]
    landed = exchange(onward)

    share = half * width // (count * 8 * 128)
    gate_out, up_out, down_out, first_in, second_in, grad_in = [
        landed[:, i * share : (i + 1) * share] for i in range(6)
    ]
    first_out, second_out, step_out = adam_update(
        from_tiles(first_in, half, width),
        from_tiles(second_in, half, width),
        from_tiles(grad_in, half, width).astype(jnp.float32),
    )
    return (
        combined,
        from_tiles(gate_out, width, half)[None],
        from_tiles(up_out, width, half)[None],
        from_tiles(down_out, half, width)[None],
        first_out[None],
        second_out[None],
        step_out[None],
    )


def solution(mesh):
    placed = (
        P(("dp", "expert"), None),
        P(("dp", "expert"), None),
        P(("dp", "expert"), None),
        P(("dp", "expert"), None),
        P(),
        P("expert", None, None),
        P("expert", None, None),
        P("expert", None, None),
        P("expert", "dp", None),
        P("expert", "dp", None),
    )
    return jax.shard_map(
        local,
        mesh=mesh,
        in_specs=placed,
        out_specs=(
            P(("dp", "expert"), None),
            P("expert", None, "dp"),
            P("expert", None, "dp"),
            P("expert", "dp", None),
            P("expert", "dp", None),
            P("expert", "dp", None),
            P("expert", "dp", None),
        ),
        check_vma=False,
    )
```

time: 871 us -> 509 us (0.58); the launches traced: 860 us -> 508 us
  local copies, waits for them, and re-layouts: 369 us -> 33.4 us
  waiting for transfers between devices: 119 us -> 396 us
  other arithmetic: 222 us -> 22.2 us
  starting transfers between devices: 108 us -> 34.4 us
  between operations: 14.7 us -> 0.89 us
    unnamed x59 -> x22, local copies, waits for them, and re-layouts: 216 us -> 6.14 us
    all_to_all x15 -> x0, other arithmetic: 175 us -> none  [the longest x3 30.7 us: relocate_state(): lax.all_to_all(ordered[2], 'expert', split_axis=0, concat_axis=0, tiled=T...]
    all_to_all x14 -> x4, waiting for transfers between devices: 119 us -> 286 us  [exchange(): lax.all_to_all(array, 'expert', split_axis=0, concat_axis=0, tiled=True)]
    ppermute x0 -> x1, waiting for transfers between devices: none -> 110 us  [local(): taken = lax.ppermute(given, 'dp', [(0, 1), (1, 0)])]
    all_to_all x14 -> x4, starting transfers between devices: 108 us -> 31.9 us  [exchange(): lax.all_to_all(array, 'expert', split_axis=0, concat_axis=0, tiled=True)]
    all_to_all x7 -> x0, local copies, waits for them, and re-layouts: 54.7 us -> none  [the longest x1 16 us: relocate_state(): lax.all_to_all(rows[1], 'expert', split_axis=0, concat_axis=0, tiled=True)]
    gather x9 -> x1, local copies, waits for them, and re-layouts: 47.2 us -> 9.78 us  [local(): onward = jnp.concatenate([spread, answered[:, out_tiles:]], axis=1)[partner]]
    another operation x4 -> x0, local copies, waits for them, and re-layouts: 14.8 us -> none  [the longest x1 7.1 us: local(): relocated[2][0]]
  transfers between devices with their start and end apart: 15 -> 5, of which waited for: 6 -> 4; matrix products, arithmetic and copies ran while one was open for 63% -> 7% of each run, Pallas kernels for 0% -> 0%
where the time goes in v1:
time: 509 us; the launch traced here: 508 us
  waiting for transfers between devices  396 us (78%)
  starting transfers between devices  34.4 us (7%)
  local copies, waits for them, and re-layouts  33.4 us (7%)
  other arithmetic  22.2 us (4%)
  matrix products  21.7 us (4%)
    all_to_all x4, waiting for transfers between devices, exchange(): lax.all_to_all(array, 'expert', split_axis=0, concat_axis=0, tiled=True)  286 us
    ppermute x1, waiting for transfers between devices, local(): taken = lax.ppermute(given, 'dp', [(0, 1), (1, 0)])  110 us
    all_to_all x4, starting transfers between devices, exchange(): lax.all_to_all(array, 'expert', split_axis=0, concat_axis=0, tiled=True)  31.9 us
  transfers between devices with their start and end apart: 5, of which 4 were waited for; matrix products, arithmetic and copies ran while one was open for 7% of the time, Pallas kernels for 0%

profile of v1, /device:TPU:1, one launch (start us, length us, event | category | flops | bytes accessed | tf_op | source)
XLA Modules:
  0.0 508.2 jit_solution(10398883019754075165)
XLA Ops:
  3.7 5.6 %convolution_convert_fusion = bf16[2048,2048]{1,0:T(8,128)(2,1)} fusion(bf16[2048,256]{1,0:T(8,128)(2,1)S(1)} %bitcast.129, bf16[128,2048]{1,0:T(8,128)(2,1)S(1)} %copy-done.6, bf16[128,2048]{1,0:T(8,128)(2,1)S(1)} %copy-done.7), kind=kOutput, calls=%fused_computation.2 | convolution fusion | flops 2153775104 | bytes 10485760 | tf_op jit(solution)/shard_map/dot_general | solution.py:93
  9.2 11.1 %all-to-all-start = ((bf16[64,32,2048]{2,1,0:T(8,128)(2,1)}), bf16[64,32,2048]{2,1,0:T(8,128)(2,1)}, u32[]{:S(2)}, u32[]{:S(2)}) async-start(bf16[64,32,2048]{2,1,0:T(8,128)(2,1)} %bitcast.120), calls=%async_computation | async-start | bytes 16777216 | tf_op jit(solution)/shard_map/all_to_all | solution.py:33
  20.4 2.2 constant_dynamic-slice_fusion.2
  30.0 96.0 %all-to-all-done = bf16[64,32,2048]{2,1,0:T(8,128)(2,1)} async-done(((bf16[64,32,2048]{2,1,0:T(8,128)(2,1)}), bf16[64,32,2048]{2,1,0:T(8,128)(2,1)}, u32[]{:S(2)}, u32[]{:S(2)}) %all-to-all-start) | async-done | bytes 8388640 | tf_op jit(solution)/shard_map/all_to_all | solution.py:33
  126.1 7.4 %all-to-all-start.1 = ((bf16[64,60,8,128]{3,2,1,0:T(8,128)(2,1)}), bf16[64,60,8,128]{3,2,1,0:T(8,128)(2,1)}, u32[]{:S(2)}, u32[]{:S(2)}) async-start(bf16[64,60,8,128]{3,2,1,0:T(8,128)(2,1)} %constant_dynamic-update-slice_fusion), calls=%async_computation.1 | async-start | bytes 15728640 | tf_op jit(solution)/shard_map/all_to_all | solution.py:33
  133.5 4.2 fusion.21
  137.8 3.4 fusion.3
  141.3 3.8 multiply_convert_fusion
  145.0 3.7 convolution_convert_fusion.2
  148.9 2.5 collective-permute-start
  151.4 3.6 convolution_convert_fusion.1
  155.1 109.8 %collective-permute-done = bf16[384,2048]{1,0:T(8,128)(2,1)S(1)} collective-permute-done((bf16[384,2048]{1,0:T(8,128)(2,1)S(1)}, bf16[384,2048]{1,0:T(8,128)(2,1)S(1)}, u32[]{:S(2)}, u32[]{:S(2)}) %collective-permute-start) | collective-permute-done | bytes 1572896 | tf_op jit(solution)/shard_map/ppermute | solution.py:123
  265.6 3.1 pad_maximum_fusion.1
  268.6 8.0 %all-to-all-start.2 = ((bf16[64,44,8,128]{3,2,1,0:T(8,128)(2,1)}), bf16[64,44,8,128]{3,2,1,0:T(8,128)(2,1)}, u32[]{:S(2)}, u32[]{:S(2)}) async-start(bf16[64,44,8,128]{3,2,1,0:T(8,128)(2,1)} %pad_maximum_fusion.1), calls=%async_computation.2 | async-start | bytes 11534336 | tf_op jit(solution)/shard_map/all_to_all | solution.py:33
  276.8 73.6 %all-to-all-done.2 = bf16[64,44,8,128]{3,2,1,0:T(8,128)(2,1)} async-done(((bf16[64,44,8,128]{3,2,1,0:T(8,128)(2,1)}), bf16[64,44,8,128]{3,2,1,0:T(8,128)(2,1)}, u32[]{:S(2)}, u32[]{:S(2)}) %all-to-all-start.2) | async-done | bytes 5767200 | tf_op jit(solution)/shard_map/all_to_all | solution.py:33
  352.0 9.0 %pad_maximum_fusion = bf16[64,72,8,128]{3,2,1,0:T(8,128)(2,1)} fusion(bf16[64,12,8,128]{3,2,1,0:T(8,128)(2,1)S(1)} %slice.51, bf16[64,60,8,128]{3,2,1,0:T(8,128)(2,1)} %all-to-all-done.1), kind=kLoop, calls=%fused_computation.1 | loop fusion | flops 4718592 | bytes 18874368 | tf_op jit(solution)/shard_map/concatenate | solution.py:139
  360.9 9.8 %gather_fusion = bf16[64,72,8,128]{3,2,1,0:T(8,128)(2,1)} fusion(bf16[64,72,8,128]{3,2,1,0:T(8,128)(2,1)} %pad_maximum_fusion, s32[1024]{0:T(1024)S(1)} %pad_clamp_fusion), kind=kCustom, calls=%fused_computation | custom fusion | bytes 18874624 | tf_op jit(solution)/shard_map/gather | solution.py:139
  370.7 5.3 %all-to-all-start.3 = ((bf16[64,72,8,128]{3,2,1,0:T(8,128)(2,1)}), bf16[64,72,8,128]{3,2,1,0:T(8,128)(2,1)}, u32[]{:S(2)}, u32[]{:S(2)}) async-start(bf16[64,72,8,128]{3,2,1,0:T(8,128)(2,1)} %gather_fusion), calls=%async_computation.3 | async-start | bytes 18874368 | tf_op jit(solution)/shard_map/all_to_all | solution.py:33
  376.0 2.5 slice.50
  378.5 1.5 convolution_convert_fusion.3
  380.1 116.2 %all-to-all-done.3 = bf16[64,72,8,128]{3,2,1,0:T(8,128)(2,1)} async-done(((bf16[64,72,8,128]{3,2,1,0:T(8,128)(2,1)}), bf16[64,72,8,128]{3,2,1,0:T(8,128)(2,1)}, u32[]{:S(2)}, u32[]{:S(2)}) %all-to-all-start.3) | async-done | bytes 9437216 | tf_op jit(solution)/shard_map/all_to_all | solution.py:33
  496.3 5.4 %fusion.20 = (bf16[64,12,8,128]{3,2,1,0:T(8,128)(2,1)S(1)}, bf16[64,12,8,128]{3,2,1,0:T(8,128)(2,1)}, bf16[64,12,8,128]{3,2,1,0:T(8,128)(2,1)}, bf16[64,12,8,128]{3,2,1,0:T(8,128)(2,1)}) fusion(bf16[64,72,8,128]{3,2,1,0:T(8,128)(2,1)} %all-to-all-done.3), kind=kLoop, calls=%fused_computation.58 | loop fusion | bytes 12582912 | tf_op jit(solution)/shard_map/slice | solution.py:144
  501.7 2.8 convert_multiply_fusion
  504.5 3.7 divide_convert_fusion
  (40 shorter events, 13.1 us)
Async XLA Ops:
  0.6 24.9 %copy-start = (bf16[1,768,2048]{2,1,0:T(8,128)(2,1)S(1)}, bf16[1,768,2048]{2,1,0:T(8,128)(2,1)}, u32[]{:S(2)}) copy-start(bf16[1,768,2048]{2,1,0:T(8,128)(2,1)} %param.17) | copy-start | bytes 9437188
  0.6 3.0 copy-start.6
  0.7 3.0 copy-start.7
  9.2 116.8 %all-to-all-start = ((bf16[64,32,2048]{2,1,0:T(8,128)(2,1)}), bf16[64,32,2048]{2,1,0:T(8,128)(2,1)}, u32[]{:S(2)}, u32[]{:S(2)}) async-start(bf16[64,32,2048]{2,1,0:T(8,128)(2,1)} %bitcast.120), calls=%async_computation | async-start | bytes 16777216 | tf_op jit(solution)/shard_map/all_to_all | solution.py:33
  25.5 1.6 copy-start.2
  25.6 3.0 copy-start.3
  126.1 142.6 %all-to-all-start.1 = ((bf16[64,60,8,128]{3,2,1,0:T(8,128)(2,1)}), bf16[64,60,8,128]{3,2,1,0:T(8,128)(2,1)}, u32[]{:S(2)}, u32[]{:S(2)}) async-start(bf16[64,60,8,128]{3,2,1,0:T(8,128)(2,1)} %constant_dynamic-update-slice_fusion), calls=%async_computation.1 | async-start | bytes 15728640 | tf_op jit(solution)/shard_map/all_to_all | solution.py:33
  133.5 4.4 copy-start.4
  137.8 3.4 copy-start.5
  148.9 116.0 %collective-permute-start = (bf16[384,2048]{1,0:T(8,128)(2,1)S(1)}, bf16[384,2048]{1,0:T(8,128)(2,1)S(1)}, u32[]{:S(2)}, u32[]{:S(2)}) collective-permute-start(bf16[384,2048]{1,0:T(8,128)(2,1)S(1)} %constant_dynamic-slice_fusion), channel_id=1, source_target_pairs={{0,64},{64,0},{1,65},{65,1},{2,66},{66,2},{3,67},{67,3},{4,68},{68... | collective-permute-start | bytes 4718600 | tf_op jit(solution)/shard_map/ppermute | solution.py:123
  268.6 8.1 %copy-start.8 = (s32[32,2]{0,1:T(2,128)S(1)}, s32[32,2]{0,1:T(2,128)}, u32[]{:S(2)}) copy-start(s32[32,2]{0,1:T(2,128)} %param.14) | copy-start | bytes 772
  268.6 81.8 %all-to-all-start.2 = ((bf16[64,44,8,128]{3,2,1,0:T(8,128)(2,1)}), bf16[64,44,8,128]{3,2,1,0:T(8,128)(2,1)}, u32[]{:S(2)}, u32[]{:S(2)}) async-start(bf16[64,44,8,128]{3,2,1,0:T(8,128)(2,1)} %pad_maximum_fusion.1), calls=%async_computation.2 | async-start | bytes 11534336 | tf_op jit(solution)/shard_map/all_to_all | solution.py:33
  370.7 125.6 %all-to-all-start.3 = ((bf16[64,72,8,128]{3,2,1,0:T(8,128)(2,1)}), bf16[64,72,8,128]{3,2,1,0:T(8,128)(2,1)}, u32[]{:S(2)}, u32[]{:S(2)}) async-start(bf16[64,72,8,128]{3,2,1,0:T(8,128)(2,1)} %gather_fusion), calls=%async_computation.3 | async-start | bytes 18874368 | tf_op jit(solution)/shard_map/all_to_all | solution.py:33
  504.5 3.7 copy-start.1

commit v2 on v1

--- a/solution.py
+++ b/solution.py
@@ -118,36 +118,36 @@
     partial = lax.dot_general(
         hidden, scaled, (((0,), (0,)), ((), ())), preferred_element_type=jnp.float32
     ).astype(jnp.bfloat16)
-    kept = lax.dynamic_slice_in_dim(partial, replica * half, half, 0)
-    given = lax.dynamic_slice_in_dim(partial, (1 - replica) * half, half, 0)
-    taken = lax.ppermute(given, "dp", [(0, 1), (1, 0)])
     outputs = jnp.dot(hidden, down_w, preferred_element_type=jnp.float32).astype(jnp.bfloat16)
-    grad = (kept.astype(jnp.float32) + taken.astype(jnp.float32)).astype(jnp.bfloat16)
-    answer = jnp.concatenate([to_tiles(outputs, count), to_tiles(grad, count)], axis=1)
-    answer, spread = lax.optimization_barrier((answer, spread))
-    answered = exchange(answer)
+    pieces = to_tiles(partial, lax.axis_size("dp") * count)
+    pieces, spread = lax.optimization_barrier((pieces, spread))
+    halves = lax.all_to_all(pieces, ("dp", "expert"), split_axis=0, concat_axis=0, tiled=True)
 
-    out_tiles = 2 * (width // 128)
-    returned = from_tiles(answered[:, :out_tiles], count * capacity, width)
+    answer = to_tiles(outputs, count)
+    moved = spread[partner]
+    share = moved.shape[1] // 5
+    onward = jnp.concatenate([answer, moved, moved[:, :share]], axis=1)
+    onward, halves = lax.optimization_barrier((onward, halves))
+    grad = jnp.sum(halves.reshape(-1, count, share, 8, 128).astype(jnp.float32), axis=0)
+    grad = grad.astype(jnp.bfloat16)[partner]
+    out_tiles = answer.shape[1]
+    onward = lax.dynamic_update_slice(onward, grad, (0, out_tiles + 5 * share, 0, 0))
+    landed = exchange(onward)
+
+    returned = from_tiles(landed[:, :out_tiles], count * capacity, width)
     combined = lax.dot_general(
         weigh.reshape(count * capacity, tok),
         returned,
         (((0,), (0,)), ((), ())),
         preferred_element_type=jnp.float32,
     ).astype(jnp.bfloat16)
-
-    onward = jnp.concatenate([spread, answered[:, out_tiles:]], axis=1)[partner]
-    landed = exchange(onward)
-
-    share = half * width // (count * 8 * 128)
     gate_out, up_out, down_out, first_in, second_in, grad_in = [
-        landed[:, i * share : (i + 1) * share] for i in range(6)
+        landed[:, out_tiles + i * share : out_tiles + (i + 1) * share] for i in range(6)
     ]
-    first_out, second_out, step_out = adam_update(
-        from_tiles(first_in, half, width),
-        from_tiles(second_in, half, width),
-        from_tiles(grad_in, half, width).astype(jnp.float32),
-    )
+    first_out, second_out, step_out = [
+        from_tiles(member, half, width)
+        for member in adam_update(first_in, second_in, grad_in.astype(jnp.float32))
+    ]
     return (
         combined,
         from_tiles(gate_out, width, half)[None],

time: 509 us -> 456 us (0.90)
  waiting for transfers between devices: 396 us -> 190 us
  blocking collectives: 0 us -> 159 us
  starting transfers between devices: 34.4 us -> 28 us
    all_to_all x0 -> x1, blocking collectives: none -> 159 us  [exchange(): lax.all_to_all(array, 'expert', split_axis=0, concat_axis=0, tiled=True)]
    ppermute x1 -> x0, waiting for transfers between devices: 110 us -> none  [local(): taken = lax.ppermute(given, 'dp', [(0, 1), (1, 0)])]
    all_to_all x4 -> x2, waiting for transfers between devices: 286 us -> 177 us  [exchange(): lax.all_to_all(array, 'expert', split_axis=0, concat_axis=0, tiled=True)]
    all_to_all x4 -> x2, starting transfers between devices: 31.9 us -> 18.5 us  [exchange(): lax.all_to_all(array, 'expert', split_axis=0, concat_axis=0, tiled=True)]
    all_to_all x0 -> x1, waiting for transfers between devices: none -> 12.8 us  [local(): lax.all_to_all(pieces, ('dp', 'expert'), split_axis=0, concat_axis=0, til...]
    all_to_all x0 -> x1, starting transfers between devices: none -> 9.49 us  [local(): lax.all_to_all(pieces, ('dp', 'expert'), split_axis=0, concat_axis=0, til...]
    slice x3 -> x4, local copies, waits for them, and re-layouts: 9.41 us -> 4.06 us  [the longest x1 2.28 us: local(): landed[:, out_tiles + i * share:out_tiles + (i + 1) * share]]
    concatenate x2 -> x1, other arithmetic: 12.1 us -> 11.5 us  [local(): onward = jnp.concatenate([answer, moved, moved[:, :share]], axis=1)]
  transfers between devices with their start and end apart: 5 -> 3, of which waited for: 4 -> 3; matrix products, arithmetic and copies ran while one was open for 7% -> 12% of each run, Pallas kernels for 0% -> 0%
where the time goes in v2:
time: 456 us; the launch traced here: 455 us
  waiting for transfers between devices  190 us (42%)
  blocking collectives  159 us (35%)
  local copies, waits for them, and re-layouts  30.3 us (7%)
  starting transfers between devices  28 us (6%)
  matrix products  25.8 us (6%)
  other arithmetic  21.4 us (5%)
    all_to_all x2, waiting for transfers between devices, exchange(): lax.all_to_all(array, 'expert', split_axis=0, concat_axis=0, tiled=True)  177 us
    all_to_all x1, blocking collectives, exchange(): lax.all_to_all(array, 'expert', split_axis=0, concat_axis=0, tiled=True)  159 us
    all_to_all x2, starting transfers between devices, exchange(): lax.all_to_all(array, 'expert', split_axis=0, concat_axis=0, tiled=True)  18.5 us
    all_to_all x1, waiting for transfers between devices, local(): lax.all_to_all(pieces, ('dp', 'expert'), split_axis=0, concat_axis=0, til...  12.8 us
    concatenate x1, other arithmetic, local(): onward = jnp.concatenate([answer, moved, moved[:, :share]], axis=1)  11.5 us
    all_to_all x1, starting transfers between devices, local(): lax.all_to_all(pieces, ('dp', 'expert'), split_axis=0, concat_axis=0, til...  9.49 us
  transfers between devices with their start and end apart: 3, of which 3 were waited for; matrix products, arithmetic and copies ran while one was open for 12% of the time, Pallas kernels for 0%

profile of v2, /device:TPU:1, one launch (start us, length us, event | category | flops | bytes accessed | tf_op | source)
XLA Modules:
  0.0 455.0 jit_solution(3242469795034817025)
XLA Ops:
  3.7 5.6 %convolution_convert_fusion = bf16[2048,2048]{1,0:T(8,128)(2,1)} fusion(bf16[2048,256]{1,0:T(8,128)(2,1)S(1)} %bitcast.114, bf16[128,2048]{1,0:T(8,128)(2,1)S(1)} %copy-done.6, bf16[128,2048]{1,0:T(8,128)(2,1)S(1)} %copy-done.7), kind=kOutput, calls=%fused_computation.3 | convolution fusion | flops 2153775104 | bytes 10485760 | tf_op jit(solution)/shard_map/dot_general | solution.py:93
  9.2 11.1 %all-to-all-start = ((bf16[64,32,2048]{2,1,0:T(8,128)(2,1)}), bf16[64,32,2048]{2,1,0:T(8,128)(2,1)}, u32[]{:S(2)}, u32[]{:S(2)}) async-start(bf16[64,32,2048]{2,1,0:T(8,128)(2,1)} %bitcast.109), calls=%async_computation | async-start | bytes 16777216 | tf_op jit(solution)/shard_map/all_to_all | solution.py:33
  20.4 2.2 constant_dynamic-slice_fusion.1
  22.6 1.5 constant_dynamic-update-slice_fusion.4
  24.1 1.5 constant_dynamic-update-slice_fusion.3
  25.7 1.5 constant_dynamic-update-slice_fusion.2
  28.7 1.5 constant_dynamic-update-slice_fusion
  30.1 95.9 %all-to-all-done = bf16[64,32,2048]{2,1,0:T(8,128)(2,1)} async-done(((bf16[64,32,2048]{2,1,0:T(8,128)(2,1)}), bf16[64,32,2048]{2,1,0:T(8,128)(2,1)}, u32[]{:S(2)}, u32[]{:S(2)}) %all-to-all-start) | async-done | bytes 8388640 | tf_op jit(solution)/shard_map/all_to_all | solution.py:33
  126.1 7.4 %all-to-all-start.1 = ((bf16[64,60,8,128]{3,2,1,0:T(8,128)(2,1)}), bf16[64,60,8,128]{3,2,1,0:T(8,128)(2,1)}, u32[]{:S(2)}, u32[]{:S(2)}) async-start(bf16[64,60,8,128]{3,2,1,0:T(8,128)(2,1)} %constant_dynamic-update-slice_fusion), calls=%async_computation.1 | async-start | bytes 15728640 | tf_op jit(solution)/shard_map/all_to_all | solution.py:33
  133.5 4.2 fusion.21
  137.8 3.4 fusion.3
  141.3 3.8 multiply_convert_fusion
  146.2 4.9 %convolution_convert_fusion.2 = bf16[768,2048]{1,0:T(8,128)(2,1)} fusion(bf16[1024,768]{1,0:T(8,128)(2,1)S(1)} %multiply_convert_fusion, bf16[1024,2048]{1,0:T(8,128)(2,1)S(1)} %bitcast.115), kind=kOutput, calls=%fused_computation.7 | convolution fusion | flops 3222798336 | bytes 8912896 | tf_op jit(solution)/shard_map/dot_general | solution.py:118
  151.1 81.2 %all-to-all-done.1 = bf16[64,60,8,128]{3,2,1,0:T(8,128)(2,1)} async-done(((bf16[64,60,8,128]{3,2,1,0:T(8,128)(2,1)}), bf16[64,60,8,128]{3,2,1,0:T(8,128)(2,1)}, u32[]{:S(2)}, u32[]{:S(2)}) %all-to-all-start.1) | async-done | bytes 7864352 | tf_op jit(solution)/shard_map/all_to_all | solution.py:33
  232.3 9.5 %all-to-all-start.2 = ((bf16[128,12,8,128]{3,2,1,0:T(8,128)(2,1)}), bf16[128,12,8,128]{3,2,1,0:T(8,128)(2,1)}, u32[]{:S(2)}, u32[]{:S(2)}) async-start(bf16[128,12,8,128]{3,2,1,0:T(8,128)(2,1)} %bitcast.119), calls=%async_computation.2 | async-start | bytes 6291456 | tf_op jit(solution)/shard_map/all_to_all | solution.py:124
  242.0 6.4 %convolution_convert_fusion.1 = bf16[1024,2048]{1,0:T(8,128)(2,1)} fusion(bf16[1024,768]{1,0:T(8,128)(2,1)} %copy-done.9, bf16[1,768,2048]{2,1,0:T(8,128)(2,1)S(1)} %copy-done), kind=kOutput, calls=%fused_computation.6 | convolution fusion | flops 3223322624 | bytes 8912896 | tf_op jit(solution)/shard_map/dot_general | solution.py:121
  248.4 8.7 %gather_fusion = bf16[64,60,8,128]{3,2,1,0:T(8,128)(2,1)} fusion(bf16[64,60,8,128]{3,2,1,0:T(8,128)(2,1)} %all-to-all-done.1, s32[1024]{0:T(1024)S(1)} %pad_clamp_fusion), kind=kCustom, calls=%fused_computation | custom fusion | bytes 15728896 | tf_op jit(solution)/shard_map/gather | solution.py:127
  258.5 11.5 %pad_maximum_fusion = bf16[64,104,8,128]{3,2,1,0:T(8,128)(2,1)} fusion(bf16[64,12,8,128]{3,2,1,0:T(8,128)(2,1)S(1)} %slice-done, bf16[64,60,8,128]{3,2,1,0:T(8,128)(2,1)} %gather_fusion, bf16[64,32,8,128]{3,2,1,0:T(8,128)(2,1)} %bitcast.118), kind=kLoop, calls=%fused_computation.2 | loop fusion | flops 13631488 | bytes 27262976 | tf_op jit(solution)/shard_map/concatenate | solution.py:129
  270.1 12.8 %all-to-all-done.2 = bf16[128,12,8,128]{3,2,1,0:T(8,128)(2,1)} async-done(((bf16[128,12,8,128]{3,2,1,0:T(8,128)(2,1)}), bf16[128,12,8,128]{3,2,1,0:T(8,128)(2,1)}, u32[]{:S(2)}, u32[]{:S(2)}) %all-to-all-start.2) | async-done | bytes 3145760 | tf_op jit(solution)/shard_map/all_to_all | solution.py:124
  282.9 3.4 reduce_sum.35
  288.6 158.6 %all_to_all.20 = bf16[64,104,8,128]{3,2,1,0:T(8,128)(2,1)S(1)} all-to-all(bf16[64,104,8,128]{3,2,1,0:T(8,128)(2,1)} %constant_dynamic-update-slice_fusion.5), channel_id=1, replica_groups=mesh['dp'=2,'expert'=64] {'expert'}, dimensions={0} | all-to-all | bytes 27262976 | tf_op jit(solution)/shard_map/all_to_all | solution.py:33
  447.6 1.5 convolution_convert_fusion.3
  449.1 3.5 divide_convert_fusion
  452.7 2.3 fusion.20
  (39 shorter events, 10.0 us)
Async XLA Ops:
  0.6 25.0 %copy-start = (bf16[1,768,2048]{2,1,0:T(8,128)(2,1)S(1)}, bf16[1,768,2048]{2,1,0:T(8,128)(2,1)}, u32[]{:S(2)}) copy-start(bf16[1,768,2048]{2,1,0:T(8,128)(2,1)} %param.17) | copy-start | bytes 9437188
  0.6 3.0 copy-start.6
  0.7 3.0 copy-start.7
  9.2 116.8 %all-to-all-start = ((bf16[64,32,2048]{2,1,0:T(8,128)(2,1)}), bf16[64,32,2048]{2,1,0:T(8,128)(2,1)}, u32[]{:S(2)}, u32[]{:S(2)}) async-start(bf16[64,32,2048]{2,1,0:T(8,128)(2,1)} %bitcast.109), calls=%async_computation | async-start | bytes 16777216 | tf_op jit(solution)/shard_map/all_to_all | solution.py:33
  25.6 1.6 copy-start.2
  25.7 3.0 copy-start.3
  126.1 106.2 %all-to-all-start.1 = ((bf16[64,60,8,128]{3,2,1,0:T(8,128)(2,1)}), bf16[64,60,8,128]{3,2,1,0:T(8,128)(2,1)}, u32[]{:S(2)}, u32[]{:S(2)}) async-start(bf16[64,60,8,128]{3,2,1,0:T(8,128)(2,1)} %constant_dynamic-update-slice_fusion), calls=%async_computation.1 | async-start | bytes 15728640 | tf_op jit(solution)/shard_map/all_to_all | solution.py:33
  133.5 4.4 copy-start.4
  137.8 3.4 copy-start.5
  145.0 1.1 copy-start.9
  232.3 9.5 %copy-start.8 = (s32[32,2]{0,1:T(2,128)S(1)}, s32[32,2]{0,1:T(2,128)}, u32[]{:S(2)}) copy-start(s32[32,2]{0,1:T(2,128)} %param.14) | copy-start | bytes 772
  232.3 50.6 %all-to-all-start.2 = ((bf16[128,12,8,128]{3,2,1,0:T(8,128)(2,1)}), bf16[128,12,8,128]{3,2,1,0:T(8,128)(2,1)}, u32[]{:S(2)}, u32[]{:S(2)}) async-start(bf16[128,12,8,128]{3,2,1,0:T(8,128)(2,1)} %bitcast.119), calls=%async_computation.2 | async-start | bytes 6291456 | tf_op jit(solution)/shard_map/all_to_all | solution.py:124
  257.1 1.4 slice-start
  449.1 5.8 %copy-start.1 = (bf16[1,768,2048]{2,1,0:T(8,128)(2,1)S(1)}, bf16[1,768,2048]{2,1,0:T(8,128)(2,1)}, u32[]{:S(2)}) copy-start(bf16[1,768,2048]{2,1,0:T(8,128)(2,1)} %param.17) | copy-start | bytes 9437188

commit v3 on v2

v3 whole, which is shorter than its diff:
```python
import jax
import jax.numpy as jnp
from jax import lax
from jax.experimental import pallas as pl
from jax.experimental.pallas import tpu as pltpu
from jax.sharding import PartitionSpec as P

beta_first = 0.9
beta_second = 0.95
adam_eps = 1e-08
capacity = 16


def partners(swap_pairs, count):
    slot_ids = jnp.arange(count, dtype=jnp.int32)
    pair_left = swap_pairs[:, 0:1]
    pair_right = swap_pairs[:, 1:2]
    offsets = jnp.where(pair_left == slot_ids[None, :], pair_right - slot_ids[None, :], 0)
    offsets = offsets + jnp.where(pair_right == slot_ids[None, :], pair_left - slot_ids[None, :], 0)
    return slot_ids + jnp.sum(offsets, axis=0)


def to_tiles(array, pieces):
    rows, columns = array.shape
    tiles = array.reshape(rows // 8, 8, columns // 128, 128).transpose(0, 2, 1, 3)
    return tiles.reshape(pieces, -1, 8, 128)


def from_tiles(tiles, rows, columns):
    split = tiles.reshape(rows // 8, columns // 128, 8, 128).transpose(0, 2, 1, 3)
    return split.reshape(rows, columns)


def exchange(array):
    return lax.all_to_all(array, "expert", split_axis=0, concat_axis=0, tiled=True)


def adam_update(first_in, second_in, grad):
    first_moment = beta_first * first_in.astype(jnp.float32) + (1.0 - beta_first) * grad
    second_moment = beta_second * second_in.astype(jnp.float32) + (1.0 - beta_second) * grad * grad
    direction = first_moment / (jnp.sqrt(second_moment) + adam_eps)
    return (
        first_moment.astype(jnp.bfloat16),
        second_moment.astype(jnp.bfloat16),
        direction.astype(jnp.bfloat16),
    )


def pack_kernel(
    replica_ref,
    routes_ref,
    gates_ref,
    tokens_ref,
    cotangent_ref,
    gate_ref,
    up_ref,
    down_ref,
    first_ref,
    second_ref,
    out_ref,
    weigh_ref,
    rank_ref,
    weight_ref,
):
    count, tok = rank_ref.shape
    dests = out_ref.shape[0]
    step = pl.program_id(0)

    @pl.when(step == 0)
    def _():
        expert_ids = lax.broadcasted_iota(jnp.int32, (count, tok), 0)
        named = jnp.zeros((count, tok), jnp.float32)
        weight = jnp.zeros((count, tok), jnp.float32)
        for k in range(routes_ref.shape[0]):
            hit = routes_ref[k : k + 1, :] == expert_ids
            named = jnp.where(hit, 1.0, named)
            weight = jnp.where(hit, gates_ref[k : k + 1, :], weight)
        earlier = lax.broadcasted_iota(jnp.int32, (tok, tok), 0) < lax.broadcasted_iota(
            jnp.int32, (tok, tok), 1
        )
        rank = jnp.dot(
            named.astype(jnp.bfloat16),
            jnp.where(earlier, 1.0, 0.0).astype(jnp.bfloat16),
            preferred_element_type=jnp.float32,
        )
        rank_ref[...] = jnp.where(named > 0.0, rank, -1.0)
        weight_ref[...] = weight

    here = pl.ds(pl.multiple_of(step * dests, dests), dests)
    rank = rank_ref[here, :]
    weight = weight_ref[here, :]
    slot_ids = lax.broadcasted_iota(jnp.int32, (capacity, tok), 0).astype(jnp.float32)
    picks, weighs = [], []
    for s in range(dests):
        chosen = rank[s : s + 1, :] == slot_ids
        picks.append(jnp.where(chosen, 1.0, 0.0))
        weighs.append(jnp.where(chosen, weight[s : s + 1, :], 0.0))
    pick = jnp.concatenate(picks, axis=0).astype(jnp.bfloat16)
    weigh = jnp.concatenate(weighs, axis=0).astype(jnp.bfloat16)
    weigh_ref[...] = weigh
    x_rows = jnp.dot(pick, tokens_ref[...], preferred_element_type=jnp.float32)
    scaled = jnp.dot(weigh, cotangent_ref[...], preferred_element_type=jnp.float32)

    def spread(source, first_slot):
        tall, wide = source.shape[0] // 8, source.shape[1] // 128
        each = tall * wide // dests
        for index in range(tall * wide):
            i, j = divmod(index, wide)
            tile = source[8 * i : 8 * i + 8, 128 * j : 128 * j + 128]
            out_ref[index // each, first_slot + index % each] = tile.astype(jnp.bfloat16)
        return first_slot + each

    slot = 0
    for ref in (gate_ref, up_ref, down_ref, first_ref, second_ref):
        slot = spread(ref, slot)
    slot = spread(x_rows, slot)
    spread(scaled, slot)


def pack(routes, route_gates, tokens, cotangent, gate_w, up_w, down_w, first, second, replica):
    count = lax.axis_size("expert")
    tok, width = tokens.shape
    half = first.shape[0]
    dests = 8
    steps = count // dests
    state_tiles = 5 * half * width // (count * 1024)
    tiles = state_tiles + 2 * capacity * width // 1024
    whole = lambda i, r: (0, 0)
    columns = lambda i, r: (i, r[0])
    own = lambda i, r: (i, 0)
    return pl.pallas_call(
        pack_kernel,
        out_shape=(
            jax.ShapeDtypeStruct((count, tiles, 8, 128), jnp.bfloat16),
            jax.ShapeDtypeStruct((count * capacity, tok), jnp.bfloat16),
        ),
        grid_spec=pltpu.PrefetchScalarGridSpec(
            num_scalar_prefetch=1,
            grid=(steps,),
            in_specs=[
                pl.BlockSpec(routes.shape, whole),
                pl.BlockSpec(route_gates.shape, whole),
                pl.BlockSpec(tokens.shape, whole),
                pl.BlockSpec(cotangent.shape, whole),
                pl.BlockSpec((width // steps, half), columns),
                pl.BlockSpec((width // steps, half), columns),
                pl.BlockSpec((half // steps, width), lambda i, r: (i + steps * r[0], 0)),
                pl.BlockSpec((half // steps, width), own),
                pl.BlockSpec((half // steps, width), own),
            ],
            out_specs=(
                pl.BlockSpec((dests, tiles, 8, 128), lambda i, r: (i, 0, 0, 0)),
                pl.BlockSpec((dests * capacity, tok), own),
            ),
            scratch_shapes=[pltpu.VMEM((count, tok), jnp.float32)] * 2,
        ),
        cost_estimate=pl.CostEstimate(
            flops=4 * count * capacity * tok * width, bytes_accessed=26_000_000, transcendentals=0
        ),
        name="pack",
    )(replica, routes, route_gates, tokens, cotangent, gate_w, up_w, down_w, first, second)


def forward_kernel(partner_ref, answer_ref, *refs):
    out_ref = refs[-1]
    out_tiles = answer_ref.shape[1]
    out_ref[:, :out_tiles] = answer_ref[...]
    for k, ref in enumerate(refs[:-1]):
        out_ref[k, out_tiles : out_tiles + ref.shape[1]] = ref[0]


def pack_onward(answer, gathered, partner, state_tiles, grad_tiles):
    count, out_tiles = answer.shape[:2]
    dests = 8

    def source(k):
        return pl.BlockSpec(
            (1, state_tiles, 8, 128), lambda i, p: (p[i * dests + k], 0, 0, 0)
        )

    tiles = out_tiles + state_tiles + grad_tiles
    return pl.pallas_call(
        forward_kernel,
        out_shape=jax.ShapeDtypeStruct((count, tiles, 8, 128), jnp.bfloat16),
        grid_spec=pltpu.PrefetchScalarGridSpec(
            num_scalar_prefetch=1,
            grid=(count // dests,),
            in_specs=[pl.BlockSpec((dests, out_tiles, 8, 128), lambda i, p: (i, 0, 0, 0))]
            + [source(k) for k in range(dests)],
            out_specs=pl.BlockSpec((dests, tiles, 8, 128), lambda i, p: (i, 0, 0, 0)),
        ),
        cost_estimate=pl.CostEstimate(flops=0, bytes_accessed=26_000_000, transcendentals=0),
        name="pack_onward",
    )(partner, answer, *([gathered] * dests))


def local(
    tokens,
    routes,
    route_gates,
    cotangent,
    swap_pairs,
    w_gate,
    w_up,
    w_down,
    moment_first,
    moment_second,
):
    count = lax.axis_size("expert")
    replica = lax.axis_index("dp")
    tok, width = tokens.shape
    gate_w, up_w, down_w = w_gate[0], w_up[0], w_down[0]
    half = gate_w.shape[1] // lax.axis_size("dp")
    share = half * width // (count * 1024)
    out_tiles = capacity * width // 1024

    packed, weigh = pack(
        routes.T,
        route_gates.T.astype(jnp.float32),
        tokens,
        cotangent,
        gate_w,
        up_w,
        down_w,
        moment_first[0],
        moment_second[0],
        replica.astype(jnp.int32).reshape(1),
    )
    spread = exchange(packed)
    spread, swap_pairs, weigh = lax.optimization_barrier((spread, swap_pairs, weigh))
    partner = partners(swap_pairs, count)

    state_tiles = 5 * share
    x_rows = from_tiles(
        spread[:, state_tiles : state_tiles + out_tiles], count * capacity, width
    )
    scaled = from_tiles(spread[:, state_tiles + out_tiles :], count * capacity, width)
    gate_pre = jnp.dot(x_rows, gate_w, preferred_element_type=jnp.float32)
    up_pre = jnp.dot(x_rows, up_w, preferred_element_type=jnp.float32)
    hidden = (jax.nn.silu(gate_pre) * up_pre).astype(jnp.bfloat16)
    partial = lax.dot_general(
        hidden, scaled, (((0,), (0,)), ((), ())), preferred_element_type=jnp.float32
    ).astype(jnp.bfloat16)
    pieces = to_tiles(partial, lax.axis_size("dp") * count)
    halves = lax.all_to_all(pieces, ("dp", "expert"), split_axis=0, concat_axis=0, tiled=True)

    outputs = jnp.dot(hidden, down_w, preferred_element_type=jnp.float32).astype(jnp.bfloat16)
    onward = pack_onward(to_tiles(outputs, count), spread, partner, state_tiles, share)
    onward, halves = lax.optimization_barrier((onward, halves))
    grad = jnp.sum(halves.reshape(-1, count, share, 8, 128).astype(jnp.float32), axis=0)
    grad = grad.astype(jnp.bfloat16)[partner]
    onward = lax.dynamic_update_slice(onward, grad, (0, out_tiles + state_tiles, 0, 0))
    landed = exchange(onward)

    returned = from_tiles(landed[:, :out_tiles], count * capacity, width)
    combined = lax.dot_general(
        weigh, returned, (((0,), (0,)), ((), ())), preferred_element_type=jnp.float32
    ).astype(jnp.bfloat16)
    gate_out, up_out, down_out, first_in, second_in, grad_in = [
        landed[:, out_tiles + i * share : out_tiles + (i + 1) * share] for i in range(6)
    ]
    first_out, second_out, step_out = [
        from_tiles(member, half, width)
        for member in adam_update(first_in, second_in, grad_in.astype(jnp.float32))
    ]
    return (
        combined,
        from_tiles(gate_out, width, half)[None],
        from_tiles(up_out, width, half)[None],
        from_tiles(down_out, half, width)[None],
        first_out[None],
        second_out[None],
        step_out[None],
    )


def solution(mesh):
    placed = (
        P(("dp", "expert"), None),
        P(("dp", "expert"), None),
        P(("dp", "expert"), None),
        P(("dp", "expert"), None),
        P(),
        P("expert", None, None),
        P("expert", None, None),
        P("expert", None, None),
        P("expert", "dp", None),
        P("expert", "dp", None),
    )
    return jax.shard_map(
        local,
        mesh=mesh,
        in_specs=placed,
        out_specs=(
            P(("dp", "expert"), None),
            P("expert", None, "dp"),
            P("expert", None, "dp"),
            P("expert", "dp", None),
            P("expert", "dp", None),
            P("expert", "dp", None),
            P("expert", "dp", None),
        ),
        check_vma=False,
    )
```

time: 456 us -> 445 us (0.976)
  blocking collectives: 159 us -> 350 us
  waiting for transfers between devices: 190 us -> 21 us
  Pallas kernels: 0 us -> 24.1 us
  starting transfers between devices: 28 us -> 5.88 us
  local copies, waits for them, and re-layouts: 30.3 us -> 13.5 us
  other arithmetic: 21.4 us -> 7.59 us
    all_to_all x1 -> x2, blocking collectives: 159 us -> 350 us  [exchange(): lax.all_to_all(array, 'expert', split_axis=0, concat_axis=0, tiled=True)]
    all_to_all x2 -> x0, waiting for transfers between devices: 177 us -> none  [exchange(): lax.all_to_all(array, 'expert', split_axis=0, concat_axis=0, tiled=True)]
    pallas_call x0 -> x2, Pallas kernels: none -> 24.1 us  [the longest x1 12.2 us: pack(): pl.pallas_call(pack_kernel, out_shape=(jax.ShapeDtypeStruct((count, tiles...]
    all_to_all x2 -> x0, starting transfers between devices: 18.5 us -> none  [exchange(): lax.all_to_all(array, 'expert', split_axis=0, concat_axis=0, tiled=True)]
    concatenate x3 -> x0, other arithmetic: 11.7 us -> none  [the longest x1 11.5 us: local(): onward = jnp.concatenate([answer, moved, moved[:, :share]], axis=1)]
    gather x1 -> x0, local copies, waits for them, and re-layouts: 8.71 us -> none  [local(): moved = spread[partner]]
    all_to_all x1, waiting for transfers between devices: 12.8 us -> 21 us  [local(): lax.all_to_all(pieces, ('dp', 'expert'), split_axis=0, concat_axis=0, til...]
    dot_general x3 -> x1, matrix products: 7.24 us -> 1.53 us  [local(): lax.dot_general(weigh, returned, (((0,), (0,)), ((), ())), preferred_elem...]
  transfers between devices with their start and end apart: 3 -> 1, of which waited for: 3 -> 1; matrix products, arithmetic and copies ran while one was open for 12% -> 2% of each run, Pallas kernels for 0% -> 3%
where the time goes in v3:
time: 445 us; the launch traced here: 444 us
  blocking collectives  350 us (79%)
  Pallas kernels  24.1 us (5%)
  matrix products  21.3 us (5%)
  waiting for transfers between devices  21 us (5%)
  local copies, waits for them, and re-layouts  13.5 us (3%)
  other arithmetic  7.59 us (2%)
  starting transfers between devices  5.88 us (1%)
    all_to_all x2, blocking collectives, exchange(): lax.all_to_all(array, 'expert', split_axis=0, concat_axis=0, tiled=True)  350 us
    all_to_all x1, waiting for transfers between devices, local(): lax.all_to_all(pieces, ('dp', 'expert'), split_axis=0, concat_axis=0, til...  21 us
    pallas_call x1, Pallas kernels, pack(): pl.pallas_call(pack_kernel, out_shape=(jax.ShapeDtypeStruct((count, tiles...  12.2 us
    pallas_call x1, Pallas kernels, pack_onward(): pl.pallas_call(forward_kernel, out_shape=jax.ShapeDtypeStruct((count, til...  11.9 us
  transfers between devices with their start and end apart: 1, of which 1 were waited for; matrix products, arithmetic and copies ran while one was open for 2% of the time, Pallas kernels for 3%

profile of v3, /device:TPU:1, one launch (start us, length us, event | category | flops | bytes accessed | tf_op | source)
XLA Modules:
  0.0 444.4 jit_solution(14300357847177818177)
XLA Ops:
  0.6 1.3 convert_bitcast_fusion.gates_ref
  1.9 12.2 %pack.1 = (bf16[64,124,8,128]{3,2,1,0:T(8,128)(2,1)}, bf16[1024,128]{1,0:T(8,128)(2,1)}) custom-call(s32[1]{0:T(128)} %bitcast.replica_ref, s32[4,128]{1,0:T(4,128)} %bitcast.106, f32[4,128]{1,0:T(4,128)} %convert_bitcast_fusion.gates_ref, bf16[128,2048]{1,0:T(8,128)(2,1)} %tokens_ref.1, bf16[128,2048]{1,0:T(8,128)(2,1)} %cotangent_ref.1, ...), custom_call_target="tpu_custom_call" | custom-call | flops 1073741824 | bytes 26000000 | tf_op jit(solution)/shard_map/pack/pallas_call | solution.py:131
  14.1 191.7 %all_to_all.15.refs_0_.refs_1_.refs_2_.refs_3_.refs_4_.refs_5_.refs_6_.refs_7_ = bf16[64,124,8,128]{3,2,1,0:T(8,128)(2,1)S(1)} all-to-all(bf16[64,124,8,128]{3,2,1,0:T(8,128)(2,1)} %get-tuple-element.14), channel_id=1, replica_groups=mesh['dp'=2,'expert'=64] {'expert'}, dimensions={0} | all-to-all | bytes 32505856 | tf_op jit(solution)/shard_map/all_to_all | solution.py:35
  205.7 1.2 fusion.9
  207.0 5.2 %copy-done = bf16[64,124,8,128]{3,2,1,0:T(8,128)(2,1)} copy-done((bf16[64,124,8,128]{3,2,1,0:T(8,128)(2,1)}, bf16[64,124,8,128]{3,2,1,0:T(8,128)(2,1)S(1)}, u32[]{:S(2)}) %copy-start) | copy-done | bytes 16252952
  212.2 3.4 fusion.7
  215.7 3.7 multiply_convert_fusion
  219.3 0.0 copy-start.5
  219.3 4.9 %convolution_convert_fusion.1 = bf16[768,2048]{1,0:T(8,128)(2,1)} fusion(bf16[1024,768]{1,0:T(8,128)(2,1)S(1)} %multiply_convert_fusion, bf16[1024,2048]{1,0:T(8,128)(2,1)S(1)} %bitcast.91), kind=kOutput, calls=%fused_computation.4 | convolution fusion | flops 3222798336 | bytes 8912896 | tf_op jit(solution)/shard_map/dot_general | solution.py:241
  224.3 5.9 %all-to-all-start.1 = ((bf16[128,12,8,128]{3,2,1,0:T(8,128)(2,1)}), bf16[128,12,8,128]{3,2,1,0:T(8,128)(2,1)S(1)}, u32[]{:S(2)}, u32[]{:S(2)}) async-start(bf16[128,12,8,128]{3,2,1,0:T(8,128)(2,1)} %bitcast.94), calls=%async_computation.1 | async-start | bytes 6291456 | tf_op jit(solution)/shard_map/all_to_all | solution.py:245
  230.2 0.1 add_reduce_fusion
  230.3 0.5 iota_add_fusion.partner_ref
  230.8 7.8 %convolution_convert_fusion = bf16[1024,2048]{1,0:T(8,128)(2,1)} fusion(bf16[1024,768]{1,0:T(8,128)(2,1)} %copy-done.5, bf16[1,768,2048]{2,1,0:T(8,128)(2,1)} %param.17), kind=kOutput, calls=%fused_computation.3 | convolution fusion | flops 3223322624 | bytes 8912896 | tf_op jit(solution)/shard_map/dot_general | solution.py:247
  238.5 11.9 %pack_onward.1 = bf16[64,104,8,128]{3,2,1,0:T(8,128)(2,1)} custom-call(s32[64]{0:T(128)} %iota_add_fusion.partner_ref, bf16[64,32,8,128]{3,2,1,0:T(8,128)(2,1)} %bitcast.90, bf16[64,124,8,128]{3,2,1,0:T(8,128)(2,1)} %copy-done, bf16[64,124,8,128]{3,2,1,0:T(8,128)(2,1)} %copy-done, bf16[64,124,8,128]{3,2,1,0:T(8,128)(2,1)} %copy-done, ...), custom_call_target="tpu_custom_call" | custom-call | bytes 26000000 | tf_op jit(solution)/shard_map/pack_onward/pallas_call | solution.py:182
  250.5 21.0 %all-to-all-done.1 = bf16[128,12,8,128]{3,2,1,0:T(8,128)(2,1)S(1)} async-done(((bf16[128,12,8,128]{3,2,1,0:T(8,128)(2,1)}), bf16[128,12,8,128]{3,2,1,0:T(8,128)(2,1)S(1)}, u32[]{:S(2)}, u32[]{:S(2)}) %all-to-all-start.1) | async-done | bytes 3145760 | tf_op jit(solution)/shard_map/all_to_all | solution.py:245
  271.5 2.2 reduce_sum.24
  273.7 2.3 gather_fusion
  275.9 1.5 constant_dynamic-update-slice_fusion
  277.4 158.6 %all_to_all.16 = bf16[64,104,8,128]{3,2,1,0:T(8,128)(2,1)S(1)} all-to-all(bf16[64,104,8,128]{3,2,1,0:T(8,128)(2,1)} %constant_dynamic-update-slice_fusion), channel_id=1, replica_groups=mesh['dp'=2,'expert'=64] {'expert'}, dimensions={0} | all-to-all | bytes 27262976 | tf_op jit(solution)/shard_map/all_to_all | solution.py:35
  436.1 0.4 slice.46
  436.4 0.6 copy-done.3
  437.0 1.5 convolution_convert_fusion.2
  438.6 3.5 divide_convert_fusion
  442.1 2.3 fusion.10
  (12 shorter events, 0.0 us)
Async XLA Ops:
  205.7 6.5 %copy-start = (bf16[64,124,8,128]{3,2,1,0:T(8,128)(2,1)}, bf16[64,124,8,128]{3,2,1,0:T(8,128)(2,1)S(1)}, u32[]{:S(2)}) copy-start(bf16[64,124,8,128]{3,2,1,0:T(8,128)(2,1)S(1)} %all_to_all.15.refs_0_.refs_1_.refs_2_.refs_3_.refs_4_.refs_5_.refs_6_.refs_7_) | copy-start | bytes 48758788
  205.7 6.5 %copy-start.1 = (bf16[1,2048,768]{2,1,0:T(8,128)(2,1)S(1)}, bf16[1,2048,768]{2,1,0:T(8,128)(2,1)}, u32[]{:S(2)}) copy-start(bf16[1,2048,768]{2,1,0:T(8,128)(2,1)} %param.15) | copy-start | bytes 9437188
  212.2 3.4 copy-start.2
  219.3 4.9 %copy-start.5 = (bf16[1024,768]{1,0:T(8,128)(2,1)}, bf16[1024,768]{1,0:T(8,128)(2,1)S(1)}, u32[]{:S(2)}) copy-start(bf16[1024,768]{1,0:T(8,128)(2,1)S(1)} %multiply_convert_fusion) | copy-start | bytes 4718596
  224.3 5.9 %copy-start.4 = (s32[32,2]{0,1:T(2,128)S(1)}, s32[32,2]{0,1:T(2,128)}, u32[]{:S(2)}) copy-start(s32[32,2]{0,1:T(2,128)} %param.14) | copy-start | bytes 772
  224.3 47.3 %all-to-all-start.1 = ((bf16[128,12,8,128]{3,2,1,0:T(8,128)(2,1)}), bf16[128,12,8,128]{3,2,1,0:T(8,128)(2,1)S(1)}, u32[]{:S(2)}, u32[]{:S(2)}) async-start(bf16[128,12,8,128]{3,2,1,0:T(8,128)(2,1)} %bitcast.94), calls=%async_computation.1 | async-start | bytes 6291456 | tf_op jit(solution)/shard_map/all_to_all | solution.py:245
  436.1 1.0 copy-start.3

commit v4 on v3

v4 whole, which is shorter than its diff:
```python
import jax
import jax.numpy as jnp
from jax import lax
from jax.experimental import pallas as pl
from jax.experimental.pallas import tpu as pltpu
from jax.sharding import PartitionSpec as P

beta_first = 0.9
beta_second = 0.95
adam_eps = 1e-08
capacity = 16


def partners(swap_pairs, count):
    slot_ids = jnp.arange(count, dtype=jnp.int32)
    pair_left = swap_pairs[:, 0:1]
    pair_right = swap_pairs[:, 1:2]
    offsets = jnp.where(pair_left == slot_ids[None, :], pair_right - slot_ids[None, :], 0)
    offsets = offsets + jnp.where(pair_right == slot_ids[None, :], pair_left - slot_ids[None, :], 0)
    return slot_ids + jnp.sum(offsets, axis=0)


def to_tiles(array, pieces):
    rows, columns = array.shape
    tiles = array.reshape(rows // 8, 8, columns // 128, 128).transpose(0, 2, 1, 3)
    return tiles.reshape(pieces, -1, 8, 128)


def from_tiles(tiles, rows, columns):
    split = tiles.reshape(rows // 8, columns // 128, 8, 128).transpose(0, 2, 1, 3)
    return split.reshape(rows, columns)


def exchange(array):
    return lax.all_to_all(array, "expert", split_axis=0, concat_axis=0, tiled=True)


def adam_update(first_in, second_in, grad):
    first_moment = beta_first * first_in.astype(jnp.float32) + (1.0 - beta_first) * grad
    second_moment = beta_second * second_in.astype(jnp.float32) + (1.0 - beta_second) * grad * grad
    direction = first_moment / (jnp.sqrt(second_moment) + adam_eps)
    return (
        first_moment.astype(jnp.bfloat16),
        second_moment.astype(jnp.bfloat16),
        direction.astype(jnp.bfloat16),
    )


def pack_kernel(
    replica_ref,
    routes_ref,
    gates_ref,
    tokens_ref,
    cotangent_ref,
    gate_ref,
    up_ref,
    down_ref,
    first_ref,
    second_ref,
    out_ref,
    weigh_ref,
    stage_ref,
    rank_ref,
    weight_ref,
    in_sems,
    row_sems,
    state_sem,
):
    count, tok = rank_ref.shape
    tiles = stage_ref.shape[1]
    rows_tiles = capacity * tokens_ref.shape[1] // 1024
    state_tiles = tiles - 2 * rows_tiles
    steps = row_sems.shape[0]
    dests = count // steps
    replica = replica_ref[0]

    loads = []

    def load(source, slot, size):
        loads.append(
            pltpu.make_async_copy(
                source, stage_ref.at[:, slot : slot + size], in_sems.at[len(loads)]
            )
        )

    slot = 0
    for ref in (gate_ref, up_ref):
        tall, wide = ref.shape[1], ref.shape[2] // 2
        for a in range(tall):
            load(ref.at[:, a, pl.ds(replica * wide, wide)], slot, wide)
            slot += wide
    share = first_ref.shape[1]
    load(down_ref.at[pl.ds(replica * count, count)], slot, share)
    load(first_ref, slot + share, share)
    load(second_ref, slot + 2 * share, share)
    for copy in loads:
        copy.start()

    expert_ids = lax.broadcasted_iota(jnp.int32, (count, tok), 0)
    named = jnp.zeros((count, tok), jnp.float32)
    weight = jnp.zeros((count, tok), jnp.float32)
    gates = gates_ref[...].astype(jnp.float32)
    for k in range(routes_ref.shape[0]):
        hit = routes_ref[k : k + 1, :] == expert_ids
        named = jnp.where(hit, 1.0, named)
        weight = jnp.where(hit, gates[k : k + 1, :], weight)
    earlier = lax.broadcasted_iota(jnp.int32, (tok, tok), 0) < lax.broadcasted_iota(
        jnp.int32, (tok, tok), 1
    )
    rank_all = jnp.dot(
        named.astype(jnp.bfloat16),
        jnp.where(earlier, 1.0, 0.0).astype(jnp.bfloat16),
        preferred_element_type=jnp.float32,
    )
    rank_ref[...] = jnp.where(named > 0.0, rank_all, -1.0)
    weight_ref[...] = weight
    slot_ids = lax.broadcasted_iota(jnp.int32, (capacity, tok), 0).astype(jnp.float32)

    state_out = pltpu.make_async_copy(
        stage_ref.at[:, :state_tiles], out_ref.at[:, :state_tiles], state_sem
    )

    def rows_out(step):
        here = pl.ds(step * dests, dests)
        return pltpu.make_async_copy(
            stage_ref.at[here, state_tiles:], out_ref.at[here, state_tiles:], row_sems.at[step]
        )

    def one_step(step, carry):
        rank = rank_ref[pl.ds(pl.multiple_of(step * dests, dests), dests), :]
        weight = weight_ref[pl.ds(pl.multiple_of(step * dests, dests), dests), :]
        picks, weighs = [], []
        for s in range(dests):
            chosen = rank[s : s + 1, :] == slot_ids
            picks.append(jnp.where(chosen, 1.0, 0.0))
            weighs.append(jnp.where(chosen, weight[s : s + 1, :], 0.0))
        pick = jnp.concatenate(picks, axis=0).astype(jnp.bfloat16)
        weigh = jnp.concatenate(weighs, axis=0).astype(jnp.bfloat16)
        weigh_ref[pl.ds(pl.multiple_of(step * dests * capacity, 128), dests * capacity), :] = weigh
        for part, (lhs, rhs) in enumerate(((pick, tokens_ref), (weigh, cotangent_ref))):
            rows = jnp.dot(lhs, rhs[...], preferred_element_type=jnp.float32)
            wide = rows.shape[1] // 128
            for index in range(dests * rows_tiles):
                i, j = divmod(index, wide)
                stage_ref[
                    step * dests + index // rows_tiles,
                    state_tiles + part * rows_tiles + index % rows_tiles,
                ] = rows[8 * i : 8 * i + 8, 128 * j : 128 * j + 128].astype(jnp.bfloat16)
        rows_out(step).start()

        @pl.when(step == steps // 2)
        def _():
            for copy in loads:
                copy.wait()
            state_out.start()

        return carry

    lax.fori_loop(0, steps, one_step, 0)

    def one_wait(step, carry):
        rows_out(step).wait()
        return carry

    lax.fori_loop(0, steps, one_wait, 0)
    state_out.wait()


def pack(routes, route_gates, tokens, cotangent, gate_w, up_w, down_w, first, second, replica):
    count = lax.axis_size("expert")
    tok, width = tokens.shape
    share = first.size // (count * 1024)
    steps = 8
    tiles = 5 * share + 2 * capacity * width // 1024

    def columns(array):
        wide = array.shape[1] // 128
        return to_tiles(array, count).reshape(count, -1, wide, 8, 128)

    vmem = pl.BlockSpec(memory_space=pltpu.VMEM)
    anywhere = pl.BlockSpec(memory_space=pl.ANY)
    gate_view, up_view = columns(gate_w), columns(up_w)
    return pl.pallas_call(
        pack_kernel,
        out_shape=(
            jax.ShapeDtypeStruct((count, tiles, 8, 128), jnp.bfloat16),
            jax.ShapeDtypeStruct((count * capacity, tok), jnp.bfloat16),
        ),
        in_specs=[pl.BlockSpec(memory_space=pltpu.SMEM)] + [vmem] * 4 + [anywhere] * 5,
        out_specs=(anywhere, vmem),
        scratch_shapes=[
            pltpu.VMEM((count, tiles, 8, 128), jnp.bfloat16),
            pltpu.VMEM((count, tok), jnp.float32),
            pltpu.VMEM((count, tok), jnp.float32),
            pltpu.SemaphoreType.DMA((2 * gate_view.shape[1] + 3,)),
            pltpu.SemaphoreType.DMA((steps,)),
            pltpu.SemaphoreType.DMA,
        ],
        cost_estimate=pl.CostEstimate(
            flops=4 * count * capacity * tok * width, bytes_accessed=26_000_000, transcendentals=0
        ),
        name="pack",
    )(
        replica,
        routes,
        route_gates,
        tokens,
        cotangent,
        gate_view,
        up_view,
        to_tiles(down_w, 2 * count),
        to_tiles(first, count),
        to_tiles(second, count),
    )


def onward_kernel(partner_ref, answer_ref, state_ref, out_ref, stage_ref, state_sems, sems):
    count, out_tiles = answer_ref.shape[:2]
    tiles = stage_ref.shape[1]

    def piece(dest):
        return pltpu.make_async_copy(
            state_ref.at[partner_ref[dest]],
            stage_ref.at[dest, out_tiles:],
            state_sems.at[dest],
        )

    def start(dest, carry):
        piece(dest).start()
        return carry

    def wait(dest, carry):
        piece(dest).wait()
        return carry

    answer = pltpu.make_async_copy(answer_ref, stage_ref.at[:, :out_tiles], sems.at[0])
    answer.start()
    lax.fori_loop(0, count, start, 0)
    answer.wait()
    lax.fori_loop(0, count, wait, 0)
    leave = pltpu.make_async_copy(stage_ref, out_ref.at[:, :tiles], sems.at[1])
    leave.start()
    leave.wait()


def pack_onward(answer, gathered, partner, state_tiles, grad_tiles):
    count, out_tiles = answer.shape[:2]
    anywhere = pl.BlockSpec(memory_space=pl.ANY)
    return pl.pallas_call(
        onward_kernel,
        out_shape=jax.ShapeDtypeStruct(
            (count, out_tiles + state_tiles + grad_tiles, 8, 128), jnp.bfloat16
        ),
        in_specs=[pl.BlockSpec(memory_space=pltpu.SMEM), anywhere, anywhere],
        out_specs=anywhere,
        scratch_shapes=[
            pltpu.VMEM((count, out_tiles + state_tiles, 8, 128), jnp.bfloat16),
            pltpu.SemaphoreType.DMA((count,)),
            pltpu.SemaphoreType.DMA((2,)),
        ],
        cost_estimate=pl.CostEstimate(flops=0, bytes_accessed=24_000_000, transcendentals=0),
        name="pack_onward",
    )(partner, answer, gathered)


def grad_kernel(partner_ref, halves_ref, onward_ref, out_ref, stage_ref, sem):
    count, share = stage_ref.shape[:2]

    def one(dest, carry):
        place = partner_ref[dest]
        total = halves_ref[place].astype(jnp.float32)
        for r in range(1, halves_ref.shape[0] // count):
            total = total + halves_ref[r * count + place].astype(jnp.float32)
        stage_ref[dest] = total.astype(jnp.bfloat16)
        return carry

    lax.fori_loop(0, count, one, 0)
    leave = pltpu.make_async_copy(stage_ref, out_ref.at[:, out_ref.shape[1] - share :], sem)
    leave.start()
    leave.wait()


def add_grad(halves, onward, partner):
    count = onward.shape[0]
    share = halves.shape[1]
    anywhere = pl.BlockSpec(memory_space=pl.ANY)
    return pl.pallas_call(
        grad_kernel,
        out_shape=jax.ShapeDtypeStruct(onward.shape, onward.dtype),
        in_specs=[
            pl.BlockSpec(memory_space=pltpu.SMEM),
            pl.BlockSpec(memory_space=pltpu.VMEM),
            anywhere,
        ],
        out_specs=anywhere,
        scratch_shapes=[
            pltpu.VMEM((count, share, 8, 128), jnp.bfloat16),
            pltpu.SemaphoreType.DMA,
        ],
        input_output_aliases={2: 0},
        cost_estimate=pl.CostEstimate(flops=0, bytes_accessed=5_000_000, transcendentals=0),
        name="add_grad",
    )(partner, pltpu.with_memory_space_constraint(halves, pltpu.VMEM), onward)


def local(
    tokens,
    routes,
    route_gates,
    cotangent,
    swap_pairs,
    w_gate,
    w_up,
    w_down,
    moment_first,
    moment_second,
):
    count = lax.axis_size("expert")
    replica = lax.axis_index("dp")
    tok, width = tokens.shape
    gate_w, up_w, down_w = w_gate[0], w_up[0], w_down[0]
    half = gate_w.shape[1] // lax.axis_size("dp")
    share = half * width // (count * 1024)
    out_tiles = capacity * width // 1024

    packed, weigh = pack(
        routes.T,
        route_gates.T,
        tokens,
        cotangent,
        gate_w,
        up_w,
        down_w,
        moment_first[0],
        moment_second[0],
        replica.astype(jnp.int32).reshape(1),
    )
    spread = exchange(packed)
    spread, swap_pairs, weigh = lax.optimization_barrier((spread, swap_pairs, weigh))
    partner = partners(swap_pairs, count)

    state_tiles = 5 * share
    x_rows = from_tiles(
        spread[:, state_tiles : state_tiles + out_tiles], count * capacity, width
    )
    scaled = from_tiles(spread[:, state_tiles + out_tiles :], count * capacity, width)
    state, x_rows, scaled = lax.optimization_barrier((spread[:, :state_tiles], x_rows, scaled))
    gate_pre = jnp.dot(x_rows, gate_w, preferred_element_type=jnp.float32)
    up_pre = jnp.dot(x_rows, up_w, preferred_element_type=jnp.float32)
    hidden = (jax.nn.silu(gate_pre) * up_pre).astype(jnp.bfloat16)
    partial = lax.dot_general(
        hidden, scaled, (((0,), (0,)), ((), ())), preferred_element_type=jnp.float32
    ).astype(jnp.bfloat16)
    pieces = to_tiles(partial, lax.axis_size("dp") * count)
    halves = lax.all_to_all(pieces, ("dp", "expert"), split_axis=0, concat_axis=0, tiled=True)

    hidden, pieces = lax.optimization_barrier((hidden, pieces))
    outputs = jnp.dot(hidden, down_w, preferred_element_type=jnp.float32).astype(jnp.bfloat16)
    onward = pack_onward(to_tiles(outputs, count), state, partner, state_tiles, share)
    onward = add_grad(halves, onward, partner)
    landed = exchange(onward)

    returned = from_tiles(landed[:, :out_tiles], count * capacity, width)
    combined = lax.dot_general(
        weigh, returned, (((0,), (0,)), ((), ())), preferred_element_type=jnp.float32
    ).astype(jnp.bfloat16)
    gate_out, up_out, down_out, first_in, second_in, grad_in = [
        landed[:, out_tiles + i * share : out_tiles + (i + 1) * share] for i in range(6)
    ]
    first_out, second_out, step_out = [
        from_tiles(member, half, width)
        for member in adam_update(first_in, second_in, grad_in.astype(jnp.float32))
    ]
    return (
        combined,
        from_tiles(gate_out, width, half)[None],
        from_tiles(up_out, width, half)[None],
        from_tiles(down_out, half, width)[None],
        first_out[None],
        second_out[None],
        step_out[None],
    )


def solution(mesh):
    placed = (
        P(("dp", "expert"), None),
        P(("dp", "expert"), None),
        P(("dp", "expert"), None),
        P(("dp", "expert"), None),
        P(),
        P("expert", None, None),
        P("expert", None, None),
        P("expert", None, None),
        P("expert", "dp", None),
        P("expert", "dp", None),
    )
    return jax.shard_map(
        local,
        mesh=mesh,
        in_specs=placed,
        out_specs=(
            P(("dp", "expert"), None),
            P("expert", None, "dp"),
            P("expert", None, "dp"),
            P("expert", "dp", None),
            P("expert", "dp", None),
            P("expert", "dp", None),
            P("expert", "dp", None),
        ),
        check_vma=False,
    )
```

time: 445 us -> 445 us (level)
    slice x0 -> x1, local copies, waits for them, and re-layouts: none -> 6.84 us  [local(): spread[:, :state_tiles]]
    unnamed x12 -> x10, local copies, waits for them, and re-layouts: 5.84 us -> 0.82 us
    pallas_call x1 -> x2, Pallas kernels: 11.9 us -> 12.9 us  [the longest x1 10.1 us: pack_onward(): pl.pallas_call(onward_kernel, out_shape=jax.ShapeDtypeStruct((count, out_...]
  transfers between devices with their start and end apart: 1 -> 1, of which waited for: 1 -> 1; matrix products, arithmetic and copies ran while one was open for 2% -> 2% of each run, Pallas kernels for 3% -> 2%
where the time goes in v4:
time: 445 us; the launch traced here: 444 us
  blocking collectives  350 us (79%)
  Pallas kernels  24.3 us (5%)
  waiting for transfers between devices  22.7 us (5%)
  matrix products  21.5 us (5%)
  local copies, waits for them, and re-layouts  14.4 us (3%)
  starting transfers between devices  5.88 us (1%)
    all_to_all x2, blocking collectives, exchange(): lax.all_to_all(array, 'expert', split_axis=0, concat_axis=0, tiled=True)  350 us
    all_to_all x1, waiting for transfers between devices, local(): lax.all_to_all(pieces, ('dp', 'expert'), split_axis=0, concat_axis=0, til...  22.7 us
    pallas_call x1, Pallas kernels, pack(): pl.pallas_call(pack_kernel, out_shape=(jax.ShapeDtypeStruct((count, tiles...  11.4 us
    pallas_call x1, Pallas kernels, pack_onward(): pl.pallas_call(onward_kernel, out_shape=jax.ShapeDtypeStruct((count, out_...  10.1 us
  transfers between devices with their start and end apart: 1, of which 1 were waited for; matrix products, arithmetic and copies ran while one was open for 2% of the time, Pallas kernels for 2%

profile of v4, /device:TPU:1, one launch (start us, length us, event | category | flops | bytes accessed | tf_op | source)
XLA Modules:
  0.0 444.1 jit_solution(9563380445883002042)
XLA Ops:
  0.6 11.4 %pack.1 = (bf16[64,124,8,128]{3,2,1,0:T(8,128)(2,1)}, bf16[1024,128]{1,0:T(8,128)(2,1)}) custom-call(s32[1]{0:T(128)} %bitcast.replica_ref, s32[4,128]{1,0:T(4,128)} %bitcast.122, bf16[4,128]{1,0:T(4,128)(2,1)} %bitcast.123, bf16[128,2048]{1,0:T(8,128)(2,1)} %tokens_ref.1, bf16[128,2048]{1,0:T(8,128)(2,1)} %cotangent_ref.1, ...), custom_call_target="tpu_custom_call" | custom-call | flops 1073741824 | bytes 26000000 | tf_op jit(solution)/shard_map/pack/pallas_call | solution.py:183
  12.0 191.8 %all_to_all.15 = bf16[64,124,8,128]{3,2,1,0:T(8,128)(2,1)} all-to-all(bf16[64,124,8,128]{3,2,1,0:T(8,128)(2,1)} %get-tuple-element.16), channel_id=1, replica_groups=mesh['dp'=2,'expert'=64] {'expert'}, dimensions={0} | all-to-all | bytes 32505856 | tf_op jit(solution)/shard_map/all_to_all | solution.py:35
  203.8 6.8 %slice.38.state_ref = bf16[64,60,8,128]{3,2,1,0:T(8,128)(2,1)} slice(bf16[64,124,8,128]{3,2,1,0:T(8,128)(2,1)} %all_to_all.15), slice={[0:64], [0:60], [0:8], [0:128]} | slice | bytes 15728640 | tf_op jit(solution)/shard_map/slice | solution.py:347
  210.6 4.1 fusion.11
  214.8 0.2 copy-done
  215.0 3.4 fusion.3
  218.4 0.0 copy-done.1
  218.4 3.8 multiply_convert_fusion
  222.2 0.0 copy-start.4
  222.2 4.9 %convolution_convert_fusion.1 = bf16[768,2048]{1,0:T(8,128)(2,1)} fusion(bf16[1024,768]{1,0:T(8,128)(2,1)S(1)} %multiply_convert_fusion, bf16[1024,2048]{1,0:T(8,128)(2,1)S(1)} %bitcast.106), kind=kOutput, calls=%fused_computation.3 | convolution fusion | flops 3222798336 | bytes 8912896 | tf_op jit(solution)/shard_map/dot_general | solution.py:351
  227.1 0.0 copy-done.4
  227.1 5.9 %all-to-all-start.1 = ((bf16[128,12,8,128]{3,2,1,0:T(8,128)(2,1)}), bf16[128,12,8,128]{3,2,1,0:T(8,128)(2,1)S(1)}, u32[]{:S(2)}, u32[]{:S(2)}) async-start(bf16[128,12,8,128]{3,2,1,0:T(8,128)(2,1)} %bitcast.110), calls=%async_computation.1 | async-start | bytes 6291456 | tf_op jit(solution)/shard_map/all_to_all | solution.py:355
  233.0 0.1 add_reduce_fusion
  233.1 0.5 iota_add_fusion.partner_ref
  233.6 7.9 %convolution_convert_fusion = bf16[1024,2048]{1,0:T(8,128)(2,1)} fusion(bf16[1024,768]{1,0:T(8,128)(2,1)} %copy-done.4, bf16[1,768,2048]{2,1,0:T(8,128)(2,1)} %param.17), kind=kOutput, calls=%fused_computation.2 | convolution fusion | flops 3223322624 | bytes 8912896 | tf_op jit(solution)/shard_map/dot_general | solution.py:358
  241.5 10.1 %pack_onward.1.onward_ref = bf16[64,104,8,128]{3,2,1,0:T(8,128)(2,1)} custom-call(s32[64]{0:T(128)} %iota_add_fusion.partner_ref, bf16[64,32,8,128]{3,2,1,0:T(8,128)(2,1)} %bitcast.109, bf16[64,60,8,128]{3,2,1,0:T(8,128)(2,1)} %slice.38.state_ref), custom_call_target="tpu_custom_call" | custom-call | bytes 24000000 | tf_op jit(solution)/shard_map/pack_onward/pallas_call | solution.py:249
  251.6 22.7 %all-to-all-done.1.halves_ref = bf16[128,12,8,128]{3,2,1,0:T(8,128)(2,1)S(1)} async-done(((bf16[128,12,8,128]{3,2,1,0:T(8,128)(2,1)}), bf16[128,12,8,128]{3,2,1,0:T(8,128)(2,1)S(1)}, u32[]{:S(2)}, u32[]{:S(2)}) %all-to-all-start.1) | async-done | bytes 3145760 | tf_op jit(solution)/shard_map/all_to_all | solution.py:355
  274.4 2.7 add_grad.1
  277.1 158.7 %all_to_all.16 = bf16[64,104,8,128]{3,2,1,0:T(8,128)(2,1)S(1)} all-to-all(bf16[64,104,8,128]{3,2,1,0:T(8,128)(2,1)} %add_grad.1), channel_id=1, replica_groups=mesh['dp'=2,'expert'=64] {'expert'}, dimensions={0} | all-to-all | bytes 27262976 | tf_op jit(solution)/shard_map/all_to_all | solution.py:35
  435.8 0.4 slice.48
  436.1 0.6 copy-done.2
  436.7 1.5 convolution_convert_fusion.2
  438.3 3.5 divide_convert_fusion
  441.8 2.3 fusion.12
  (6 shorter events, 0.0 us)
Async XLA Ops:
  210.6 4.4 copy-start
  215.0 3.4 copy-start.1
  222.2 4.9 %copy-start.4 = (bf16[1024,768]{1,0:T(8,128)(2,1)}, bf16[1024,768]{1,0:T(8,128)(2,1)S(1)}, u32[]{:S(2)}) copy-start(bf16[1024,768]{1,0:T(8,128)(2,1)S(1)} %multiply_convert_fusion) | copy-start | bytes 4718596
  227.1 5.9 %copy-start.3 = (s32[32,2]{0,1:T(2,128)S(1)}, s32[32,2]{0,1:T(2,128)}, u32[]{:S(2)}) copy-start(s32[32,2]{0,1:T(2,128)} %param.14) | copy-start | bytes 772
  227.1 47.3 %all-to-all-start.1 = ((bf16[128,12,8,128]{3,2,1,0:T(8,128)(2,1)}), bf16[128,12,8,128]{3,2,1,0:T(8,128)(2,1)S(1)}, u32[]{:S(2)}, u32[]{:S(2)}) async-start(bf16[128,12,8,128]{3,2,1,0:T(8,128)(2,1)} %bitcast.110), calls=%async_computation.1 | async-start | bytes 6291456 | tf_op jit(solution)/shard_map/all_to_all | solution.py:355
  435.8 1.0 copy-start.2

commit v5 on v4

--- a/solution.py
+++ b/solution.py
@@ -9,6 +9,7 @@
 beta_second = 0.95
 adam_eps = 1e-08
 capacity = 16
+vmem_limit = 24 * 1024 * 1024
 
 
 def partners(swap_pairs, count):
@@ -48,10 +49,10 @@
 
 def pack_kernel(
     replica_ref,
-    routes_ref,
-    gates_ref,
-    tokens_ref,
-    cotangent_ref,
+    routes_hbm,
+    gates_hbm,
+    tokens_hbm,
+    cotangent_hbm,
     gate_ref,
     up_ref,
     down_ref,
@@ -59,19 +60,32 @@
     second_ref,
     out_ref,
     weigh_ref,
-    stage_ref,
+    routes_ref,
+    gates_ref,
+    tokens_ref,
+    cotangent_ref,
     rank_ref,
     weight_ref,
+    row_sems,
     in_sems,
-    row_sems,
-    state_sem,
 ):
     count, tok = rank_ref.shape
-    tiles = stage_ref.shape[1]
+    rows_in = [
+        pltpu.make_async_copy(source, target, row_sems.at[n])
+        for n, (source, target) in enumerate(
+            (
+                (routes_hbm, routes_ref),
+                (gates_hbm, gates_ref),
+                (tokens_hbm, tokens_ref),
+                (cotangent_hbm, cotangent_ref),
+            )
+        )
+    ]
+    for copy in rows_in:
+        copy.start()
     rows_tiles = capacity * tokens_ref.shape[1] // 1024
-    state_tiles = tiles - 2 * rows_tiles
-    steps = row_sems.shape[0]
-    dests = count // steps
+    state_tiles = out_ref.shape[1] - 2 * rows_tiles
+    dests = 8
     replica = replica_ref[0]
 
     loads = []
@@ -79,7 +93,7 @@
     def load(source, slot, size):
         loads.append(
             pltpu.make_async_copy(
-                source, stage_ref.at[:, slot : slot + size], in_sems.at[len(loads)]
+                source, out_ref.at[:, slot : slot + size], in_sems.at[len(loads)]
             )
         )
 
@@ -96,6 +110,8 @@
     for copy in loads:
         copy.start()
 
+    for copy in rows_in[:2]:
+        copy.wait()
     expert_ids = lax.broadcasted_iota(jnp.int32, (count, tok), 0)
     named = jnp.zeros((count, tok), jnp.float32)
     weight = jnp.zeros((count, tok), jnp.float32)
@@ -115,16 +131,8 @@
     rank_ref[...] = jnp.where(named > 0.0, rank_all, -1.0)
     weight_ref[...] = weight
     slot_ids = lax.broadcasted_iota(jnp.int32, (capacity, tok), 0).astype(jnp.float32)
-
-    state_out = pltpu.make_async_copy(
-        stage_ref.at[:, :state_tiles], out_ref.at[:, :state_tiles], state_sem
-    )
-
-    def rows_out(step):
-        here = pl.ds(step * dests, dests)
-        return pltpu.make_async_copy(
-            stage_ref.at[here, state_tiles:], out_ref.at[here, state_tiles:], row_sems.at[step]
-        )
+    for copy in rows_in[2:]:
+        copy.wait()
 
     def one_step(step, carry):
         rank = rank_ref[pl.ds(pl.multiple_of(step * dests, dests), dests), :]
@@ -142,35 +150,21 @@
             wide = rows.shape[1] // 128
             for index in range(dests * rows_tiles):
                 i, j = divmod(index, wide)
-                stage_ref[
+                out_ref[
                     step * dests + index // rows_tiles,
                     state_tiles + part * rows_tiles + index % rows_tiles,
                 ] = rows[8 * i : 8 * i + 8, 128 * j : 128 * j + 128].astype(jnp.bfloat16)
-        rows_out(step).start()
-
-        @pl.when(step == steps // 2)
-        def _():
-            for copy in loads:
-                copy.wait()
-            state_out.start()
-
         return carry
 
-    lax.fori_loop(0, steps, one_step, 0)
-
-    def one_wait(step, carry):
-        rows_out(step).wait()
-        return carry
-
-    lax.fori_loop(0, steps, one_wait, 0)
-    state_out.wait()
+    lax.fori_loop(0, count // dests, one_step, 0)
+    for copy in loads:
+        copy.wait()
 
 
 def pack(routes, route_gates, tokens, cotangent, gate_w, up_w, down_w, first, second, replica):
     count = lax.axis_size("expert")
     tok, width = tokens.shape
     share = first.size // (count * 1024)
-    steps = 8
     tiles = 5 * share + 2 * capacity * width // 1024
 
     def columns(array):
@@ -183,35 +177,76 @@
     return pl.pallas_call(
         pack_kernel,
         out_shape=(
-            jax.ShapeDtypeStruct((count, tiles, 8, 128), jnp.bfloat16),
+            pltpu.VMEM((count, tiles, 8, 128), jnp.bfloat16),
             jax.ShapeDtypeStruct((count * capacity, tok), jnp.bfloat16),
         ),
-        in_specs=[pl.BlockSpec(memory_space=pltpu.SMEM)] + [vmem] * 4 + [anywhere] * 5,
-        out_specs=(anywhere, vmem),
+        in_specs=[pl.BlockSpec(memory_space=pltpu.SMEM)] + [anywhere] * 9,
+        out_specs=(vmem, vmem),
         scratch_shapes=[
-            pltpu.VMEM((count, tiles, 8, 128), jnp.bfloat16),
+            pltpu.VMEM(routes.shape, routes.dtype),
+            pltpu.VMEM(route_gates.shape, route_gates.dtype),
+            pltpu.VMEM(tokens.shape, tokens.dtype),
+            pltpu.VMEM(cotangent.shape, cotangent.dtype),
             pltpu.VMEM((count, tok), jnp.float32),
             pltpu.VMEM((count, tok), jnp.float32),
+            pltpu.SemaphoreType.DMA((4,)),
             pltpu.SemaphoreType.DMA((2 * gate_view.shape[1] + 3,)),
-            pltpu.SemaphoreType.DMA((steps,)),
-            pltpu.SemaphoreType.DMA,
         ],
         cost_estimate=pl.CostEstimate(
             flops=4 * count * capacity * tok * width, bytes_accessed=26_000_000, transcendentals=0
         ),
+        compiler_params=pltpu.CompilerParams(vmem_limit_bytes=vmem_limit),
         name="pack",
     )(
         replica,
-        routes,
-        route_gates,
-        tokens,
-        cotangent,
-        gate_view,
-        up_view,
-        to_tiles(down_w, 2 * count),
-        to_tiles(first, count),
-        to_tiles(second, count),
-    )
+        *[
+            pltpu.with_memory_space_constraint(member, pltpu.HBM)
+            for member in (
+                routes,
+                route_gates,
+                tokens,
+                cotangent,
+                gate_view,
+                up_view,
+                to_tiles(down_w, 2 * count),
+                to_tiles(first, count),
+                to_tiles(second, count),
+            )
+        ],
+    )
+
+
+def rows_kernel(landed_ref, x_ref, scaled_ref, sems):
+    out_tiles = x_ref.shape[1]
+    state_tiles = landed_ref.shape[1] - 2 * out_tiles
+    copies = [
+        pltpu.make_async_copy(
+            landed_ref.at[:, state_tiles + n * out_tiles : state_tiles + (n + 1) * out_tiles],
+            target,
+            sems.at[n],
+        )
+        for n, target in enumerate((x_ref, scaled_ref))
+    ]
+    for copy in copies:
+        copy.start()
+    for copy in copies:
+        copy.wait()
+
+
+def take_rows(landed, out_tiles):
+    count = landed.shape[0]
+    vmem = pl.BlockSpec(memory_space=pltpu.VMEM)
+    rows = pltpu.VMEM((count, out_tiles, 8, 128), jnp.bfloat16)
+    return pl.pallas_call(
+        rows_kernel,
+        out_shape=(rows, rows),
+        in_specs=[pl.BlockSpec(memory_space=pl.ANY)],
+        out_specs=(vmem, vmem),
+        scratch_shapes=[pltpu.SemaphoreType.DMA((2,))],
+        compiler_params=pltpu.CompilerParams(vmem_limit_bytes=vmem_limit),
+        cost_estimate=pl.CostEstimate(flops=0, bytes_accessed=8_400_000, transcendentals=0),
+        name="take_rows",
+    )(pltpu.with_memory_space_constraint(landed, pltpu.HBM))
 
 
 def onward_kernel(partner_ref, answer_ref, state_ref, out_ref, stage_ref, state_sems, sems):
@@ -220,7 +255,7 @@
 
     def piece(dest):
         return pltpu.make_async_copy(
-            state_ref.at[partner_ref[dest]],
+            state_ref.at[partner_ref[dest], : tiles - out_tiles],
             stage_ref.at[dest, out_tiles:],
             state_sems.at[dest],
         )
@@ -260,7 +295,7 @@
         ],
         cost_estimate=pl.CostEstimate(flops=0, bytes_accessed=24_000_000, transcendentals=0),
         name="pack_onward",
-    )(partner, answer, gathered)
+    )(partner, answer, pltpu.with_memory_space_constraint(gathered, pltpu.HBM))
 
 
 def grad_kernel(partner_ref, halves_ref, onward_ref, out_ref, stage_ref, sem):
@@ -340,11 +375,9 @@
     partner = partners(swap_pairs, count)
 
     state_tiles = 5 * share
-    x_rows = from_tiles(
-        spread[:, state_tiles : state_tiles + out_tiles], count * capacity, width
-    )
-    scaled = from_tiles(spread[:, state_tiles + out_tiles :], count * capacity, width)
-    state, x_rows, scaled = lax.optimization_barrier((spread[:, :state_tiles], x_rows, scaled))
+    x_tiles, scaled_tiles = take_rows(spread, out_tiles)
+    x_rows = from_tiles(x_tiles, count * capacity, width)
+    scaled = from_tiles(scaled_tiles, count * capacity, width)
     gate_pre = jnp.dot(x_rows, gate_w, preferred_element_type=jnp.float32)
     up_pre = jnp.dot(x_rows, up_w, preferred_element_type=jnp.float32)
     hidden = (jax.nn.silu(gate_pre) * up_pre).astype(jnp.bfloat16)
@@ -356,7 +389,7 @@
 
     hidden, pieces = lax.optimization_barrier((hidden, pieces))
     outputs = jnp.dot(hidden, down_w, preferred_element_type=jnp.float32).astype(jnp.bfloat16)
-    onward = pack_onward(to_tiles(outputs, count), state, partner, state_tiles, share)
+    onward = pack_onward(to_tiles(outputs, count), spread, partner, state_tiles, share)
     onward = add_grad(halves, onward, partner)
     landed = exchange(onward)
 

time: 445 us -> 432 us (0.971)
  local copies, waits for them, and re-layouts: 14.4 us -> 3.39 us
    slice x2 -> x0, local copies, waits for them, and re-layouts: 11 us -> none  [the longest x1 6.84 us: local(): spread[:, :state_tiles]]
    pallas_call x1 -> x2, Pallas kernels: 11.4 us -> 10.3 us  [the longest x1 6.68 us: pack(): pl.pallas_call(pack_kernel, out_shape=(pltpu.VMEM((count, tiles, 8, 128),...]
where the time goes in v5:
time: 432 us
  blocking collectives  350 us (81%)
  Pallas kernels  23.1 us (5%)
  waiting for transfers between devices  22.9 us (5%)
  matrix products  21.3 us (5%)
  starting transfers between devices  5.87 us (1%)
    all_to_all x2, blocking collectives, exchange(): lax.all_to_all(array, 'expert', split_axis=0, concat_axis=0, tiled=True)  350 us
    all_to_all x1, waiting for transfers between devices, local(): lax.all_to_all(pieces, ('dp', 'expert'), split_axis=0, concat_axis=0, til...  22.9 us
    pallas_call x1, Pallas kernels, pack_onward(): pl.pallas_call(onward_kernel, out_shape=jax.ShapeDtypeStruct((count, out_...  10 us
  transfers between devices with their start and end apart: 1, of which 1 were waited for; matrix products, arithmetic and copies ran while one was open for 2% of the time, Pallas kernels for 2%

profile of v5, /device:TPU:1, one launch (start us, length us, event | category | flops | bytes accessed | tf_op | source)
XLA Modules:
  0.0 431.9 jit_solution(9049201575799000052)
XLA Ops:
  0.6 6.7 %pack.1 = (bf16[64,124,8,128]{3,2,1,0:T(8,128)(2,1)S(1)}, bf16[1024,128]{1,0:T(8,128)(2,1)S(1)}) custom-call(s32[1]{0:T(128)} %bitcast.replica_ref, s32[4,128]{1,0:T(4,128)} %bitcast.122, bf16[4,128]{1,0:T(4,128)(2,1)} %bitcast.123, bf16[128,2048]{1,0:T(8,128)(2,1)} %tokens_hbm.1, bf16[128,2048]{1,0:T(8,128)(2,1)} %cotangent_hbm.1, ...), custom_call_target="tpu_custom_call" | custom-call | flops 1073741824 | bytes 26000000 | tf_op jit(solution)/shard_map/pack/pallas_call | solution.py:177
  7.3 191.6 %all_to_all.15.landed_ref.state_ref = bf16[64,124,8,128]{3,2,1,0:T(8,128)(2,1)} all-to-all(bf16[64,124,8,128]{3,2,1,0:T(8,128)(2,1)S(1)} %get-tuple-element.15), channel_id=1, replica_groups=mesh['dp'=2,'expert'=64] {'expert'}, dimensions={0} | all-to-all | bytes 32505856 | tf_op jit(solution)/shard_map/all_to_all | solution.py:36
  198.9 0.0 copy-start
  198.9 3.6 take_rows.1
  202.5 0.7 copy-done
  203.2 3.4 fusion.3
  206.7 0.0 copy-done.1
  206.7 3.7 multiply_convert_fusion
  210.4 0.0 copy-start.3
  210.4 4.9 %convolution_convert_fusion.1 = bf16[768,2048]{1,0:T(8,128)(2,1)} fusion(bf16[1024,768]{1,0:T(8,128)(2,1)S(1)} %multiply_convert_fusion, bf16[1024,2048]{1,0:T(8,128)(2,1)S(1)} %bitcast.105), kind=kOutput, calls=%fused_computation.3 | convolution fusion | flops 3222798336 | bytes 8912896 | tf_op jit(solution)/shard_map/dot_general | solution.py:384
  215.3 0.0 copy-done.3
  215.3 5.9 %all-to-all-start.1 = ((bf16[128,12,8,128]{3,2,1,0:T(8,128)(2,1)}), bf16[128,12,8,128]{3,2,1,0:T(8,128)(2,1)S(1)}, u32[]{:S(2)}, u32[]{:S(2)}) async-start(bf16[128,12,8,128]{3,2,1,0:T(8,128)(2,1)} %bitcast.110), calls=%async_computation.1 | async-start | bytes 6291456 | tf_op jit(solution)/shard_map/all_to_all | solution.py:388
  221.1 0.0 copy-done.2
  221.2 0.1 add_reduce_fusion
  221.3 0.5 iota_add_fusion.partner_ref
  221.8 7.8 %convolution_convert_fusion = bf16[1024,2048]{1,0:T(8,128)(2,1)} fusion(bf16[1024,768]{1,0:T(8,128)(2,1)} %copy-done.3, bf16[1,768,2048]{2,1,0:T(8,128)(2,1)} %param.17), kind=kOutput, calls=%fused_computation.2 | convolution fusion | flops 3223322624 | bytes 8912896 | tf_op jit(solution)/shard_map/dot_general | solution.py:391
  229.5 10.0 %pack_onward.1.onward_ref = bf16[64,104,8,128]{3,2,1,0:T(8,128)(2,1)} custom-call(s32[64]{0:T(128)} %iota_add_fusion.partner_ref, bf16[64,32,8,128]{3,2,1,0:T(8,128)(2,1)} %bitcast.109, bf16[64,124,8,128]{3,2,1,0:T(8,128)(2,1)} %all_to_all.15.landed_ref.state_ref), custom_call_target="tpu_custom_call" | custom-call | bytes 24000000 | tf_op jit(solution)/shard_map/pack_onward/pallas_call | solution.py:284
  239.6 22.9 %all-to-all-done.1.halves_ref = bf16[128,12,8,128]{3,2,1,0:T(8,128)(2,1)S(1)} async-done(((bf16[128,12,8,128]{3,2,1,0:T(8,128)(2,1)}), bf16[128,12,8,128]{3,2,1,0:T(8,128)(2,1)S(1)}, u32[]{:S(2)}, u32[]{:S(2)}) %all-to-all-start.1) | async-done | bytes 3145760 | tf_op jit(solution)/shard_map/all_to_all | solution.py:388
  262.5 2.8 add_grad.1
  265.3 158.8 %all_to_all.16 = bf16[64,104,8,128]{3,2,1,0:T(8,128)(2,1)S(1)} all-to-all(bf16[64,104,8,128]{3,2,1,0:T(8,128)(2,1)} %add_grad.1), channel_id=1, replica_groups=mesh['dp'=2,'expert'=64] {'expert'}, dimensions={0} | all-to-all | bytes 27262976 | tf_op jit(solution)/shard_map/all_to_all | solution.py:36
  424.1 0.4 slice.36
  424.5 1.5 convolution_convert_fusion.2
  426.1 3.5 divide_convert_fusion
  429.6 2.3 fusion.11
  (3 shorter events, 0.0 us)
Async XLA Ops:
  198.9 4.3 %copy-start = (bf16[1,2048,768]{2,1,0:T(8,128)(2,1)S(1)}, bf16[1,2048,768]{2,1,0:T(8,128)(2,1)}, u32[]{:S(2)}) copy-start(bf16[1,2048,768]{2,1,0:T(8,128)(2,1)} %param.16) | copy-start | bytes 9437188
  203.2 3.4 copy-start.1
  210.4 4.9 %copy-start.3 = (bf16[1024,768]{1,0:T(8,128)(2,1)}, bf16[1024,768]{1,0:T(8,128)(2,1)S(1)}, u32[]{:S(2)}) copy-start(bf16[1024,768]{1,0:T(8,128)(2,1)S(1)} %multiply_convert_fusion) | copy-start | bytes 4718596
  215.3 5.9 %copy-start.2 = (s32[32,2]{0,1:T(2,128)S(1)}, s32[32,2]{0,1:T(2,128)}, u32[]{:S(2)}) copy-start(s32[32,2]{0,1:T(2,128)} %param.14) | copy-start | bytes 772
  215.3 47.3 %all-to-all-start.1 = ((bf16[128,12,8,128]{3,2,1,0:T(8,128)(2,1)}), bf16[128,12,8,128]{3,2,1,0:T(8,128)(2,1)S(1)}, u32[]{:S(2)}, u32[]{:S(2)}) async-start(bf16[128,12,8,128]{3,2,1,0:T(8,128)(2,1)} %bitcast.110), calls=%async_computation.1 | async-start | bytes 6291456 | tf_op jit(solution)/shard_map/all_to_all | solution.py:388

commit v6 on v5

--- a/solution.py
+++ b/solution.py
@@ -85,7 +85,7 @@
         copy.start()
     rows_tiles = capacity * tokens_ref.shape[1] // 1024
     state_tiles = out_ref.shape[1] - 2 * rows_tiles
-    dests = 8
+    dests = 32
     replica = replica_ref[0]
 
     loads = []
@@ -219,13 +219,19 @@
 def rows_kernel(landed_ref, x_ref, scaled_ref, sems):
     out_tiles = x_ref.shape[1]
     state_tiles = landed_ref.shape[1] - 2 * out_tiles
+    parts = sems.shape[1]
+    each = x_ref.shape[0] // parts
     copies = [
         pltpu.make_async_copy(
-            landed_ref.at[:, state_tiles + n * out_tiles : state_tiles + (n + 1) * out_tiles],
-            target,
-            sems.at[n],
+            landed_ref.at[
+                part * each : (part + 1) * each,
+                state_tiles + n * out_tiles : state_tiles + (n + 1) * out_tiles,
+            ],
+            target.at[part * each : (part + 1) * each],
+            sems.at[n, part],
         )
         for n, target in enumerate((x_ref, scaled_ref))
+        for part in range(parts)
     ]
     for copy in copies:
         copy.start()
@@ -242,7 +248,7 @@
         out_shape=(rows, rows),
         in_specs=[pl.BlockSpec(memory_space=pl.ANY)],
         out_specs=(vmem, vmem),
-        scratch_shapes=[pltpu.SemaphoreType.DMA((2,))],
+        scratch_shapes=[pltpu.SemaphoreType.DMA((2, 8))],
         compiler_params=pltpu.CompilerParams(vmem_limit_bytes=vmem_limit),
         cost_estimate=pl.CostEstimate(flops=0, bytes_accessed=8_400_000, transcendentals=0),
         name="take_rows",
@@ -298,8 +304,10 @@
     )(partner, answer, pltpu.with_memory_space_constraint(gathered, pltpu.HBM))
 
 
-def grad_kernel(partner_ref, halves_ref, onward_ref, out_ref, stage_ref, sem):
+def grad_kernel(partner_ref, halves_ref, onward_ref, out_ref, stage_ref, sems):
     count, share = stage_ref.shape[:2]
+    chunks = sems.shape[0]
+    each = count // chunks
 
     def one(dest, carry):
         place = partner_ref[dest]
@@ -309,10 +317,18 @@
         stage_ref[dest] = total.astype(jnp.bfloat16)
         return carry
 
-    lax.fori_loop(0, count, one, 0)
-    leave = pltpu.make_async_copy(stage_ref, out_ref.at[:, out_ref.shape[1] - share :], sem)
-    leave.start()
-    leave.wait()
+    leaves = []
+    for chunk in range(chunks):
+        here = slice(chunk * each, (chunk + 1) * each)
+        lax.fori_loop(chunk * each, (chunk + 1) * each, one, 0, unroll=4)
+        leaves.append(
+            pltpu.make_async_copy(
+                stage_ref.at[here], out_ref.at[here, out_ref.shape[1] - share :], sems.at[chunk]
+            )
+        )
+        leaves[-1].start()
+    for leave in leaves:
+        leave.wait()
 
 
 def add_grad(halves, onward, partner):
@@ -330,12 +346,98 @@
         out_specs=anywhere,
         scratch_shapes=[
             pltpu.VMEM((count, share, 8, 128), jnp.bfloat16),
-            pltpu.SemaphoreType.DMA,
+            pltpu.SemaphoreType.DMA((4,)),
         ],
         input_output_aliases={2: 0},
         cost_estimate=pl.CostEstimate(flops=0, bytes_accessed=5_000_000, transcendentals=0),
         name="add_grad",
     )(partner, pltpu.with_memory_space_constraint(halves, pltpu.VMEM), onward)
+
+
+def update_kernel(
+    landed_ref,
+    gate_ref,
+    up_ref,
+    down_ref,
+    first_ref,
+    second_ref,
+    step_ref,
+    stage_ref,
+    weight_sems,
+    state_sems,
+):
+    count, share = gate_ref.shape[:2]
+    slot = landed_ref.shape[1] - 6 * share
+    chunks = state_sems.shape[1]
+    each = count // chunks
+    weights = [
+        pltpu.make_async_copy(
+            landed_ref.at[:, slot + n * share : slot + (n + 1) * share], target, weight_sems.at[n]
+        )
+        for n, target in enumerate((gate_ref, up_ref, down_ref))
+    ]
+    for copy in weights:
+        copy.start()
+
+    def leave(n, chunk):
+        here = pl.ds(chunk * each, each)
+        target = (first_ref, second_ref, step_ref)[n]
+        return pltpu.make_async_copy(
+            stage_ref.at[n, here], target.at[here], state_sems.at[n, chunk]
+        )
+
+    def one_piece(piece, carry):
+        first_in, second_in, grad = [
+            landed_ref[piece, slot + n * share : slot + (n + 1) * share] for n in (3, 4, 5)
+        ]
+        for n, member in enumerate(adam_update(first_in, second_in, grad.astype(jnp.float32))):
+            stage_ref[n, piece] = member
+        return carry
+
+    def two_pieces(chunk):
+        def both(pair, carry):
+            one_piece(chunk * each + 2 * pair, carry)
+            return one_piece(chunk * each + 2 * pair + 1, carry)
+
+        return both
+
+    def one_chunk(chunk, carry):
+        lax.fori_loop(0, each // 2, two_pieces(chunk), 0)
+        for n in range(3):
+            leave(n, chunk).start()
+        return carry
+
+    def one_wait(chunk, carry):
+        for n in range(3):
+            leave(n, chunk).wait()
+        return carry
+
+    lax.fori_loop(0, chunks, one_chunk, 0)
+    lax.fori_loop(0, chunks, one_wait, 0)
+    for copy in weights:
+        copy.wait()
+
+
+def update(landed, share):
+    count = landed.shape[0]
+    anywhere = pl.BlockSpec(memory_space=pl.ANY)
+    piece = jax.ShapeDtypeStruct((count, share, 8, 128), jnp.bfloat16)
+    return pl.pallas_call(
+        update_kernel,
+        out_shape=(piece,) * 6,
+        in_specs=[pl.BlockSpec(memory_space=pltpu.VMEM)],
+        out_specs=(anywhere,) * 6,
+        scratch_shapes=[
+            pltpu.VMEM((3, count, share, 8, 128), jnp.bfloat16),
+            pltpu.SemaphoreType.DMA((3,)),
+            pltpu.SemaphoreType.DMA((3, 8)),
+        ],
+        compiler_params=pltpu.CompilerParams(vmem_limit_bytes=vmem_limit),
+        cost_estimate=pl.CostEstimate(
+            flops=20_000_000, bytes_accessed=9_500_000, transcendentals=1_600_000
+        ),
+        name="update",
+    )(pltpu.with_memory_space_constraint(landed, pltpu.VMEM))
 
 
 def local(
@@ -397,21 +499,15 @@
     combined = lax.dot_general(
         weigh, returned, (((0,), (0,)), ((), ())), preferred_element_type=jnp.float32
     ).astype(jnp.bfloat16)
-    gate_out, up_out, down_out, first_in, second_in, grad_in = [
-        landed[:, out_tiles + i * share : out_tiles + (i + 1) * share] for i in range(6)
-    ]
-    first_out, second_out, step_out = [
-        from_tiles(member, half, width)
-        for member in adam_update(first_in, second_in, grad_in.astype(jnp.float32))
-    ]
+    gate_out, up_out, down_out, first_out, second_out, step_out = update(landed, share)
     return (
         combined,
         from_tiles(gate_out, width, half)[None],
         from_tiles(up_out, width, half)[None],
         from_tiles(down_out, half, width)[None],
-        first_out[None],
-        second_out[None],
-        step_out[None],
+        from_tiles(first_out, half, width)[None],
+        from_tiles(second_out, half, width)[None],
+        from_tiles(step_out, half, width)[None],
     )
 
 

time: 432 us -> 429 us (level)
  no operation moved by 1% of the time
where the time goes in v6:
time: 429 us; the launch traced here: 428 us
  blocking collectives  350 us (82%)
  Pallas kernels  25.3 us (6%)
  waiting for transfers between devices  22.9 us (5%)
  matrix products  21.3 us (5%)
  starting transfers between devices  5.88 us (1%)
    all_to_all x2, blocking collectives, exchange(): lax.all_to_all(array, 'expert', split_axis=0, concat_axis=0, tiled=True)  350 us
    all_to_all x1, waiting for transfers between devices, local(): lax.all_to_all(pieces, ('dp', 'expert'), split_axis=0, concat_axis=0, til...  22.9 us
    pallas_call x1, Pallas kernels, pack_onward(): pl.pallas_call(onward_kernel, out_shape=jax.ShapeDtypeStruct((count, out_...  10.1 us
  transfers between devices with their start and end apart: 1, of which 1 were waited for; matrix products, arithmetic and copies ran while one was open for 2% of the time, Pallas kernels for 2%

profile of v6, /device:TPU:1, one launch (start us, length us, event | category | flops | bytes accessed | tf_op | source)
XLA Modules:
  0.0 428.3 jit_solution(17581634961437058498)
XLA Ops:
  0.6 5.8 %pack.1 = (bf16[64,124,8,128]{3,2,1,0:T(8,128)(2,1)S(1)}, bf16[1024,128]{1,0:T(8,128)(2,1)S(1)}) custom-call(s32[1]{0:T(128)} %bitcast.replica_ref, s32[4,128]{1,0:T(4,128)} %bitcast.116, bf16[4,128]{1,0:T(4,128)(2,1)} %bitcast.117, bf16[128,2048]{1,0:T(8,128)(2,1)} %tokens_hbm.1, bf16[128,2048]{1,0:T(8,128)(2,1)} %cotangent_hbm.1, ...), custom_call_target="tpu_custom_call" | custom-call | flops 1073741824 | bytes 26000000 | tf_op jit(solution)/shard_map/pack/pallas_call | solution.py:177
  6.4 191.6 %all_to_all.15.landed_ref.state_ref = bf16[64,124,8,128]{3,2,1,0:T(8,128)(2,1)} all-to-all(bf16[64,124,8,128]{3,2,1,0:T(8,128)(2,1)S(1)} %get-tuple-element.21), channel_id=1, replica_groups=mesh['dp'=2,'expert'=64] {'expert'}, dimensions={0} | all-to-all | bytes 32505856 | tf_op jit(solution)/shard_map/all_to_all | solution.py:36
  198.0 3.7 take_rows.1
  201.6 0.7 copy-done
  202.3 0.0 copy-start.1
  202.3 3.4 fusion.1
  205.7 0.0 copy-done.1
  205.8 3.7 multiply_convert_fusion
  209.5 0.0 copy-start.3
  209.5 4.9 %convolution_convert_fusion.1 = bf16[768,2048]{1,0:T(8,128)(2,1)} fusion(bf16[1024,768]{1,0:T(8,128)(2,1)S(1)} %multiply_convert_fusion, bf16[1024,2048]{1,0:T(8,128)(2,1)S(1)} %bitcast.105), kind=kOutput, calls=%fused_computation.1 | convolution fusion | flops 3222798336 | bytes 8912896 | tf_op jit(solution)/shard_map/dot_general | solution.py:486
  214.4 0.0 copy-done.3
  214.4 0.0 copy-start.2
  214.4 5.9 %all-to-all-start.1 = ((bf16[128,12,8,128]{3,2,1,0:T(8,128)(2,1)}), bf16[128,12,8,128]{3,2,1,0:T(8,128)(2,1)S(1)}, u32[]{:S(2)}, u32[]{:S(2)}) async-start(bf16[128,12,8,128]{3,2,1,0:T(8,128)(2,1)} %bitcast.110), calls=%async_computation.1 | async-start | bytes 6291456 | tf_op jit(solution)/shard_map/all_to_all | solution.py:490
  220.3 0.0 copy-done.2
  220.3 0.1 add_reduce_fusion
  220.4 0.5 iota_add_fusion.partner_ref
  220.9 7.8 %convolution_convert_fusion = bf16[1024,2048]{1,0:T(8,128)(2,1)} fusion(bf16[1024,768]{1,0:T(8,128)(2,1)} %copy-done.3, bf16[1,768,2048]{2,1,0:T(8,128)(2,1)} %param.17), kind=kOutput, calls=%fused_computation | convolution fusion | flops 3223322624 | bytes 8912896 | tf_op jit(solution)/shard_map/dot_general | solution.py:493
  228.7 10.1 %pack_onward.1.onward_ref = bf16[64,104,8,128]{3,2,1,0:T(8,128)(2,1)} custom-call(s32[64]{0:T(128)} %iota_add_fusion.partner_ref, bf16[64,32,8,128]{3,2,1,0:T(8,128)(2,1)} %bitcast.109, bf16[64,124,8,128]{3,2,1,0:T(8,128)(2,1)} %all_to_all.15.landed_ref.state_ref), custom_call_target="tpu_custom_call" | custom-call | bytes 24000000 | tf_op jit(solution)/shard_map/pack_onward/pallas_call | solution.py:290
  238.8 22.9 %all-to-all-done.1.halves_ref = bf16[128,12,8,128]{3,2,1,0:T(8,128)(2,1)S(1)} async-done(((bf16[128,12,8,128]{3,2,1,0:T(8,128)(2,1)}), bf16[128,12,8,128]{3,2,1,0:T(8,128)(2,1)S(1)}, u32[]{:S(2)}, u32[]{:S(2)}) %all-to-all-start.1) | async-done | bytes 3145760 | tf_op jit(solution)/shard_map/all_to_all | solution.py:490
  261.7 2.0 add_grad.1
  263.7 158.7 %all_to_all.16.landed_ref = bf16[64,104,8,128]{3,2,1,0:T(8,128)(2,1)S(1)} all-to-all(bf16[64,104,8,128]{3,2,1,0:T(8,128)(2,1)} %add_grad.1), channel_id=1, replica_groups=mesh['dp'=2,'expert'=64] {'expert'}, dimensions={0} | all-to-all | bytes 27262976 | tf_op jit(solution)/shard_map/all_to_all | solution.py:36
  422.4 0.4 slice.12
  422.7 1.5 convolution_convert_fusion.2
  424.3 3.8 update.1
  (2 shorter events, 0.0 us)
Async XLA Ops:
  198.0 4.4 %copy-start = (bf16[1,2048,768]{2,1,0:T(8,128)(2,1)S(1)}, bf16[1,2048,768]{2,1,0:T(8,128)(2,1)}, u32[]{:S(2)}) copy-start(bf16[1,2048,768]{2,1,0:T(8,128)(2,1)} %param.16) | copy-start | bytes 9437188
  202.3 3.4 copy-start.1
  209.5 4.9 %copy-start.3 = (bf16[1024,768]{1,0:T(8,128)(2,1)}, bf16[1024,768]{1,0:T(8,128)(2,1)S(1)}, u32[]{:S(2)}) copy-start(bf16[1024,768]{1,0:T(8,128)(2,1)S(1)} %multiply_convert_fusion) | copy-start | bytes 4718596
  214.4 5.9 %copy-start.2 = (s32[32,2]{0,1:T(2,128)S(1)}, s32[32,2]{0,1:T(2,128)}, u32[]{:S(2)}) copy-start(s32[32,2]{0,1:T(2,128)} %param.14) | copy-start | bytes 772
  214.4 47.2 %all-to-all-start.1 = ((bf16[128,12,8,128]{3,2,1,0:T(8,128)(2,1)}), bf16[128,12,8,128]{3,2,1,0:T(8,128)(2,1)S(1)}, u32[]{:S(2)}, u32[]{:S(2)}) async-start(bf16[128,12,8,128]{3,2,1,0:T(8,128)(2,1)} %bitcast.110), calls=%async_computation.1 | async-start | bytes 6291456 | tf_op jit(solution)/shard_map/all_to_all | solution.py:490

commit v7 on v6

--- a/solution.py
+++ b/solution.py
@@ -216,43 +216,50 @@
     )
 
 
-def rows_kernel(landed_ref, x_ref, scaled_ref, sems):
+def split_kernel(landed_ref, x_ref, scaled_ref, state_ref, sems):
     out_tiles = x_ref.shape[1]
-    state_tiles = landed_ref.shape[1] - 2 * out_tiles
-    parts = sems.shape[1]
+    state_tiles = state_ref.shape[1]
+    parts = sems.shape[0]
     each = x_ref.shape[0] // parts
     copies = [
         pltpu.make_async_copy(
-            landed_ref.at[
-                part * each : (part + 1) * each,
-                state_tiles + n * out_tiles : state_tiles + (n + 1) * out_tiles,
-            ],
-            target.at[part * each : (part + 1) * each],
-            sems.at[n, part],
-        )
-        for n, target in enumerate((x_ref, scaled_ref))
+            landed_ref.at[part * each : (part + 1) * each, :state_tiles],
+            state_ref.at[part * each : (part + 1) * each],
+            sems.at[part],
+        )
         for part in range(parts)
     ]
     for copy in copies:
         copy.start()
+
+    def rows(block, carry):
+        x_ref[block] = landed_ref[block, state_tiles : state_tiles + out_tiles]
+        scaled_ref[block] = landed_ref[block, state_tiles + out_tiles :]
+        return carry
+
+    lax.fori_loop(0, x_ref.shape[0], rows, 0, unroll=2)
     for copy in copies:
         copy.wait()
 
 
-def take_rows(landed, out_tiles):
-    count = landed.shape[0]
+def split(landed, out_tiles):
+    count, tiles = landed.shape[:2]
     vmem = pl.BlockSpec(memory_space=pltpu.VMEM)
     rows = pltpu.VMEM((count, out_tiles, 8, 128), jnp.bfloat16)
     return pl.pallas_call(
-        rows_kernel,
-        out_shape=(rows, rows),
-        in_specs=[pl.BlockSpec(memory_space=pl.ANY)],
-        out_specs=(vmem, vmem),
-        scratch_shapes=[pltpu.SemaphoreType.DMA((2, 8))],
+        split_kernel,
+        out_shape=(
+            rows,
+            rows,
+            pltpu.HBM((count, tiles - 2 * out_tiles, 8, 128), jnp.bfloat16),
+        ),
+        in_specs=[vmem],
+        out_specs=(vmem, vmem, pl.BlockSpec(memory_space=pl.ANY)),
+        scratch_shapes=[pltpu.SemaphoreType.DMA((4,))],
         compiler_params=pltpu.CompilerParams(vmem_limit_bytes=vmem_limit),
         cost_estimate=pl.CostEstimate(flops=0, bytes_accessed=8_400_000, transcendentals=0),
-        name="take_rows",
-    )(pltpu.with_memory_space_constraint(landed, pltpu.HBM))
+        name="split",
+    )(pltpu.with_memory_space_constraint(landed, pltpu.VMEM))
 
 
 def onward_kernel(partner_ref, answer_ref, state_ref, out_ref, stage_ref, state_sems, sems):
@@ -261,7 +268,7 @@
 
     def piece(dest):
         return pltpu.make_async_copy(
-            state_ref.at[partner_ref[dest], : tiles - out_tiles],
+            state_ref.at[partner_ref[dest]],
             stage_ref.at[dest, out_tiles:],
             state_sems.at[dest],
         )
@@ -477,7 +484,7 @@
     partner = partners(swap_pairs, count)
 
     state_tiles = 5 * share
-    x_tiles, scaled_tiles = take_rows(spread, out_tiles)
+    x_tiles, scaled_tiles, state = split(spread, out_tiles)
     x_rows = from_tiles(x_tiles, count * capacity, width)
     scaled = from_tiles(scaled_tiles, count * capacity, width)
     gate_pre = jnp.dot(x_rows, gate_w, preferred_element_type=jnp.float32)
@@ -491,7 +498,7 @@
 
     hidden, pieces = lax.optimization_barrier((hidden, pieces))
     outputs = jnp.dot(hidden, down_w, preferred_element_type=jnp.float32).astype(jnp.bfloat16)
-    onward = pack_onward(to_tiles(outputs, count), spread, partner, state_tiles, share)
+    onward = pack_onward(to_tiles(outputs, count), state, partner, state_tiles, share)
     onward = add_grad(halves, onward, partner)
     landed = exchange(onward)
 

time: 429 us -> 428 us (level)
  no operation moved by 1% of the time
where the time goes in v7:
time: 428 us
  blocking collectives  350 us (82%)
  Pallas kernels  25.4 us (6%)
  waiting for transfers between devices  22.8 us (5%)
  matrix products  21.4 us (5%)
  starting transfers between devices  5.87 us (1%)
    all_to_all x2, blocking collectives, exchange(): lax.all_to_all(array, 'expert', split_axis=0, concat_axis=0, tiled=True)  350 us
    all_to_all x1, waiting for transfers between devices, local(): lax.all_to_all(pieces, ('dp', 'expert'), split_axis=0, concat_axis=0, til...  22.8 us
    pallas_call x1, Pallas kernels, pack_onward(): pl.pallas_call(onward_kernel, out_shape=jax.ShapeDtypeStruct((count, out_...  10.1 us
  transfers between devices with their start and end apart: 1, of which 1 were waited for; matrix products, arithmetic and copies ran while one was open for 2% of the time, Pallas kernels for 2%

profile of v7, /device:TPU:1, one launch (start us, length us, event | category | flops | bytes accessed | tf_op | source)
XLA Modules:
  0.0 427.9 jit_solution(6653721692053231287)
XLA Ops:
  0.6 5.8 %pack.1 = (bf16[64,124,8,128]{3,2,1,0:T(8,128)(2,1)S(1)}, bf16[1024,128]{1,0:T(8,128)(2,1)S(1)}) custom-call(s32[1]{0:T(128)} %bitcast.replica_ref, s32[4,128]{1,0:T(4,128)} %bitcast.116, bf16[4,128]{1,0:T(4,128)(2,1)} %bitcast.117, bf16[128,2048]{1,0:T(8,128)(2,1)} %tokens_hbm.1, bf16[128,2048]{1,0:T(8,128)(2,1)} %cotangent_hbm.1, ...), custom_call_target="tpu_custom_call" | custom-call | flops 1073741824 | bytes 26000000 | tf_op jit(solution)/shard_map/pack/pallas_call | solution.py:177
  6.4 191.5 %all_to_all.15.landed_ref = bf16[64,124,8,128]{3,2,1,0:T(8,128)(2,1)S(1)} all-to-all(bf16[64,124,8,128]{3,2,1,0:T(8,128)(2,1)S(1)} %get-tuple-element.22), channel_id=1, replica_groups=mesh['dp'=2,'expert'=64] {'expert'}, dimensions={0} | all-to-all | bytes 32505856 | tf_op jit(solution)/shard_map/all_to_all | solution.py:36
  197.9 0.0 copy-start
  197.9 3.7 split.1
  201.6 0.5 copy-done
  202.1 0.0 copy-start.1
  202.1 3.4 fusion.1
  205.5 0.0 copy-done.1
  205.5 3.7 multiply_convert_fusion
  209.2 0.0 copy-start.3
  209.2 4.9 %convolution_convert_fusion.1 = bf16[768,2048]{1,0:T(8,128)(2,1)} fusion(bf16[1024,768]{1,0:T(8,128)(2,1)S(1)} %multiply_convert_fusion, bf16[1024,2048]{1,0:T(8,128)(2,1)S(1)} %bitcast.105), kind=kOutput, calls=%fused_computation.1 | convolution fusion | flops 3222798336 | bytes 8912896 | tf_op jit(solution)/shard_map/dot_general | solution.py:493
  214.1 0.0 copy-done.3
  214.1 5.9 %all-to-all-start.1 = ((bf16[128,12,8,128]{3,2,1,0:T(8,128)(2,1)}), bf16[128,12,8,128]{3,2,1,0:T(8,128)(2,1)S(1)}, u32[]{:S(2)}, u32[]{:S(2)}) async-start(bf16[128,12,8,128]{3,2,1,0:T(8,128)(2,1)} %bitcast.110), calls=%async_computation.1 | async-start | bytes 6291456 | tf_op jit(solution)/shard_map/all_to_all | solution.py:497
  220.0 0.0 copy-done.2
  220.0 0.1 add_reduce_fusion
  220.1 0.5 iota_add_fusion.partner_ref
  220.6 7.8 %convolution_convert_fusion = bf16[1024,2048]{1,0:T(8,128)(2,1)} fusion(bf16[1024,768]{1,0:T(8,128)(2,1)} %copy-done.3, bf16[1,768,2048]{2,1,0:T(8,128)(2,1)} %param.17), kind=kOutput, calls=%fused_computation | convolution fusion | flops 3223322624 | bytes 8912896 | tf_op jit(solution)/shard_map/dot_general | solution.py:500
  228.4 10.1 %pack_onward.1.onward_ref = bf16[64,104,8,128]{3,2,1,0:T(8,128)(2,1)} custom-call(s32[64]{0:T(128)} %iota_add_fusion.partner_ref, bf16[64,32,8,128]{3,2,1,0:T(8,128)(2,1)} %bitcast.109, bf16[64,60,8,128]{3,2,1,0:T(8,128)(2,1)} %get-tuple-element.30.state_ref), custom_call_target="tpu_custom_call" | custom-call | bytes 24000000 | tf_op jit(solution)/shard_map/pack_onward/pallas_call | solution.py:297
  238.5 22.8 %all-to-all-done.1.halves_ref = bf16[128,12,8,128]{3,2,1,0:T(8,128)(2,1)S(1)} async-done(((bf16[128,12,8,128]{3,2,1,0:T(8,128)(2,1)}), bf16[128,12,8,128]{3,2,1,0:T(8,128)(2,1)S(1)}, u32[]{:S(2)}, u32[]{:S(2)}) %all-to-all-start.1) | async-done | bytes 3145760 | tf_op jit(solution)/shard_map/all_to_all | solution.py:497
  261.3 2.0 add_grad.1
  263.4 158.7 %all_to_all.16.landed_ref = bf16[64,104,8,128]{3,2,1,0:T(8,128)(2,1)S(1)} all-to-all(bf16[64,104,8,128]{3,2,1,0:T(8,128)(2,1)} %add_grad.1), channel_id=1, replica_groups=mesh['dp'=2,'expert'=64] {'expert'}, dimensions={0} | all-to-all | bytes 27262976 | tf_op jit(solution)/shard_map/all_to_all | solution.py:36
  422.0 0.4 slice.12
  422.4 1.5 convolution_convert_fusion.2
  424.0 3.8 update.1
  (2 shorter events, 0.0 us)
Async XLA Ops:
  197.9 4.2 copy-start
  202.1 3.4 copy-start.1
  209.2 4.9 %copy-start.3 = (bf16[1024,768]{1,0:T(8,128)(2,1)}, bf16[1024,768]{1,0:T(8,128)(2,1)S(1)}, u32[]{:S(2)}) copy-start(bf16[1024,768]{1,0:T(8,128)(2,1)S(1)} %multiply_convert_fusion) | copy-start | bytes 4718596
  214.1 5.9 %copy-start.2 = (s32[32,2]{0,1:T(2,128)S(1)}, s32[32,2]{0,1:T(2,128)}, u32[]{:S(2)}) copy-start(s32[32,2]{0,1:T(2,128)} %param.14) | copy-start | bytes 772
  214.1 47.2 %all-to-all-start.1 = ((bf16[128,12,8,128]{3,2,1,0:T(8,128)(2,1)}), bf16[128,12,8,128]{3,2,1,0:T(8,128)(2,1)S(1)}, u32[]{:S(2)}, u32[]{:S(2)}) async-start(bf16[128,12,8,128]{3,2,1,0:T(8,128)(2,1)} %bitcast.110), calls=%async_computation.1 | async-start | bytes 6291456 | tf_op jit(solution)/shard_map/all_to_all | solution.py:497
